TPU v7x, 256 devices: a whole 4x4x8 slice. The times are simulated.
256 devices in a mesh: dp: 128 (over y, z, x), rep: 2 (over core).
Axes of the slice: x: 4, y: 4, z: 8, core: 2. Of those that a mesh axis runs over, the one named last changes fastest.
Arguments:
- embeddings: float32 [131072, 1024], P(('dp', 'rep')), may hold values from -6 to 6
- cluster_ids: int32 [131072, 1], P(('dp', 'rep')), may hold values from 0 to 255; in each aligned block of 512 rows (0 to 511, 512 to 1023, ...) at most 4 rows name the same one
- boundary_slots: int32 [256, 2, 256], P(('dp', 'rep')), may hold values from 0 to 1023
Outputs:
- member_max: float32 [256, 1024], P(('dp', 'rep'))
- centrality: float32 [256, 1024], P(('dp', 'rep'))
Inputs may be any that keep to these rules, and one draw needn't show every extreme that they name: `cluster_ids`: among the rows of one device, at most 4 name the same cluster, a bound that some block reaches of them; every cluster is named by some row.
All inputs are finite; a program needn't handle non-finite values.
Results may differ from a plain program's by a relative error of at most 0.0024.
Values may be sent and summed in bfloat16 or wider, within the bound.
A program may use at most 64 MiB of HBM per device.

v0:
```python
import jax
import jax.numpy as jnp
from jax import lax
from jax.sharding import PartitionSpec as P

SLOTS = 1024


eps = 1e-06


def from_behind(array, axis, by):
    peers = lax.axis_size(axis)
    pairs = [(i, i + by) for i in range(peers) if 0 <= i + by < peers]
    return lax.ppermute(array, axis, pairs)


def per_device(embeddings, cluster_ids, boundary_slots):
    n_chips = lax.axis_size("dp")
    n_cores = lax.axis_size("rep")
    owners = n_chips * n_cores
    width = embeddings.shape[1]
    slots = SLOTS
    capacity = slots // owners
    bound = boundary_slots.shape[2]
    me = lax.axis_index(("dp", "rep"))
    labels = cluster_ids[:, 0]
    member_of = labels[:, None] == jnp.arange(owners, dtype=jnp.int32)[None, :]
    running = jnp.cumsum(member_of.astype(jnp.int32), axis=0)
    ranks = jnp.sum(jnp.where(member_of, running, 0), axis=1) - 1
    targets = labels * capacity + ranks
    unit_full = embeddings * lax.rsqrt(
        jnp.sum(embeddings * embeddings, axis=1, keepdims=True) + eps
    )
    unit_half = unit_full.astype(jnp.bfloat16)
    outgoing = jnp.zeros((slots, width), jnp.bfloat16).at[targets].set(unit_half)
    member_half = member_of.astype(jnp.bfloat16)
    shaped = outgoing.reshape(n_chips, n_cores, capacity, width)
    arrived = lax.all_to_all(
        lax.all_to_all(shaped, "dp", split_axis=0, concat_axis=0, tiled=True),
        "rep",
        split_axis=1,
        concat_axis=1,
        tiled=True,
    )
    members = arrived.reshape(slots, width)
    partial_sums = lax.dot_general(
        member_half, unit_half, (((0,), (0,)), ((), ())), preferred_element_type=jnp.float32
    )
    total = lax.psum(partial_sums, ("dp", "rep"))
    own_sum = lax.dynamic_slice_in_dim(total, me, 1, 0)
    direction = own_sum[0] * lax.rsqrt(jnp.sum(own_sum * own_sum) + eps)
    lengths = jnp.einsum("se,se->s", members, members, preferred_element_type=jnp.float32)
    filled = lengths > 0.5
    filled_int = filled.astype(jnp.int32)
    count = jnp.sum(filled_int)
    order = jnp.argsort(1 - filled_int, stable=True)
    picks = boundary_slots[0] % count
    positions = order[picks.reshape(-1)]
    outward = members[positions]
    lower = from_behind(outward[bound:], ("dp", "rep"), 1)
    upper = from_behind(outward[:bound], ("dp", "rep"), -1)
    candidates = jnp.concatenate([members, lower, upper], axis=0)
    cand_ok = jnp.concatenate(
        [filled, jnp.full((bound,), me > 0), jnp.full((bound,), me < owners - 1)]
    )
    column = jnp.arange(slots + 2 * bound, dtype=jnp.int32)
    block = min(512, slots)

    def one_block(start):
        block_rows = lax.dynamic_slice_in_dim(members, start, block, 0)
        scores = lax.dot_general(
            block_rows, candidates, (((1,), (1,)), ((), ())), preferred_element_type=jnp.float32
        )
        row_pos = start + jnp.arange(block, dtype=jnp.int32)
        keep = cand_ok[None, :] & (column[None, :] != row_pos[:, None])
        return jnp.max(jnp.where(keep, scores, -1.0), axis=1)

    starts = jnp.arange(slots // block, dtype=jnp.int32) * block
    best = lax.map(one_block, starts).reshape(slots)
    member_max = jnp.where(filled, best, 0.0)
    central = jnp.dot(
        members, direction, precision=lax.Precision.HIGHEST, preferred_element_type=jnp.float32
    )
    centrality = jnp.where(filled, central, 0.0)
    return (member_max[None, :], centrality[None, :])


def solution(mesh):
    placed = (P(("dp", "rep"), None), P(("dp", "rep"), None), P(("dp", "rep"), None, None))
    return jax.shard_map(
        per_device,
        mesh=mesh,
        in_specs=placed,
        out_specs=(P(("dp", "rep"), None), P(("dp", "rep"), None)),
        check_vma=False,
    )
```

profile of v0, /device:TPU:8, one launch (start us, length us, event | category | flops | bytes accessed | tf_op | source)
XLA Modules:
  0.0 374.8 jit_solution(14825172263603566123)
XLA Ops:
  7.2 0.0 copy-start.1
  7.2 1.8 multiply_reduce_fusion
  9.0 0.0 copy-start
  9.0 0.0 copy-done.1
  9.0 0.1 copy.12
  9.1 0.2 fusion.10
  9.4 0.1 copy.13
  9.5 0.2 fusion.9
  9.8 0.8 copy-done
  10.6 4.2 %scatter_custom_fusion = bf16[1024,1024]{1,0:T(8,128)(2,1)} fusion(s32[512]{0:T(512)S(1)} %bitcast.58, bf16[]{:T(256)} %constant.27.clone.1, f32[512,1024]{1,0:T(8,128)S(1)} %copy-done, f32[512]{0:T(512)S(1)} %add_rsqrt_fusion), kind=kCustom, calls=%fused_computation.16 | custom fusion | flops 1048576 | bytes 4196354 | tf_op jit(solution)/shard_map/scatter | solution.py:36
  14.7 4.1 %reshape.106 = bf16[128,2,4,1024]{3,2,1,0:T(4,128)(2,1)} reshape(bf16[1024,1024]{1,0:T(8,128)(2,1)} %scatter_custom_fusion) | data formatting | bytes 4194304 | tf_op jit(solution)/shard_map/reshape | solution.py:38
  18.8 15.9 %all-to-all-start = ((bf16[128,2,4,1024]{3,2,1,0:T(4,128)(2,1)}), bf16[128,2,4,1024]{3,2,1,0:T(4,128)(2,1)}, u32[]{:S(2)}, u32[]{:S(2)}) async-start(bf16[128,2,4,1024]{3,2,1,0:T(4,128)(2,1)} %reshape.106), calls=%async_computation | async-start | bytes 4194304 | tf_op jit(solution)/shard_map/all_to_all | solution.py:40
  34.8 0.0 all-reduce.2.cloned.1.call-start
  34.8 1.7 fusion.12
  36.5 0.0 all-reduce.2.cloned.1.call-update
  36.5 268.0 %all-reduce.2.cloned.1.call-done = f32[256,1024]{1,0:T(8,128)} async-done(((f32[256,1024]{1,0:T(8,128)}), f32[256,1024]{1,0:T(8,128)}) %all-reduce.2.cloned.1.call-update) | async-done | bytes 1048592 | tf_op jit(solution)/shard_map/psum | solution.py:50
  304.5 1.4 multiply_reduce_fusion.1
  306.6 0.0 all-to-all-done
  306.6 2.3 copy.14
  308.9 5.4 %all_to_all.10 = bf16[128,2,4,1024]{3,2,0,1:T(4,128)(2,1)S(1)} all-to-all(bf16[128,2,4,1024]{3,2,0,1:T(4,128)(2,1)S(1)} %copy.14), channel_id=1, replica_groups=mesh['dp'=128,'rep'=2] {'rep'}, dimensions={1} | all-to-all | bytes 4194304 | tf_op jit(solution)/shard_map/all_to_all | solution.py:39
  314.3 2.6 copy.15
  317.0 2.5 reshape.107
  319.5 0.0 copy-start.2
  319.5 0.5 fusion.6
  320.0 2.5 fusion.15
  322.5 0.6 broadcast_select_fusion
  323.1 0.6 convert_reduce_fusion
  325.0 0.0 copy-done.2
  325.0 0.1 remainder_bitcast_fusion
  325.2 4.4 %sort.17 = (s32[1024]{0:T(1024)}, s32[1024]{0:T(1024)S(1)}) sort(s32[1024]{0:T(1024)S(1)} %get-tuple-element.73, s32[1024]{0:T(1024)S(1)} %iota.25), dimensions={0}, to_apply=%region_5.6 | sort | flops 10240 | bytes 16384 | tf_op jit(solution)/shard_map/jit(argsort)/sort | solution.py:57
  329.6 2.3 gather_fusion
  331.9 2.1 gather_fusion.1
  334.0 1.1 fusion.21
  335.0 2.0 collective-permute-start
  337.1 7.7 %collective-permute-start.1 = (bf16[256,1024]{1,0:T(8,128)(2,1)}, bf16[256,1024]{1,0:T(8,128)(2,1)S(1)}, u32[]{:S(2)}, u32[]{:S(2)}) collective-permute-start(bf16[256,1024]{1,0:T(8,128)(2,1)} %get-tuple-element.71), channel_id=1, source_target_pairs={{1,0},{2,1},{3,2},{4,3},{5,4},{6,5},{7,6},{8,7},{9,8},{10,9},{11,1... | collective-permute-start | bytes 1572872 | tf_op jit(solution)/shard_map/ppermute | solution.py:15
  344.9 5.1 %collective-permute-done = bf16[256,1024]{1,0:T(8,128)(2,1)S(1)} collective-permute-done((bf16[256,1024]{1,0:T(8,128)(2,1)}, bf16[256,1024]{1,0:T(8,128)(2,1)S(1)}, u32[]{:S(2)}, u32[]{:S(2)}) %collective-permute-start) | collective-permute-done | bytes 524320 | tf_op jit(solution)/shard_map/ppermute | solution.py:15
  349.9 1.9 collective-permute-done.1
  351.8 1.9 pad_maximum_fusion
  353.7 13.6 %while.11 = (s32[]{:T(128)}, f32[2,512]{1,0:T(2,128)S(1)}, pred[1536]{0:T(1024)(128)(4,1)S(1)}, s32[2]{0:T(128)S(1)}, bf16[1024,1024]{1,0:T(8,128)(2,1)S(1)}, /*...) while((s32[]{:T(128)}, f32[2,512]{1,0:T(2,128)S(1)}, ...), condition=%wide.region_9.10_spmd.clone, body=%wide.region_7.9_spmd.clone.sunk | while | flops 1613758464 | bytes 4206743 | solution.py:80
  353.7 0.5 dynamic_slice.23
  355.9 0.5 iota_add_fusion.2
  356.4 4.0 %fusion.29 = f32[512]{0:T(512)S(1)} fusion(bf16[1536,1024]{1,0:T(8,128)(2,1)} %get-tuple-element.134, s32[512]{0:T(512)S(1)} %iota_add_fusion.2, pred[1536]{0:T(1024)(128)(4,1)S(1)} %get-tuple-element.131, bf16[1024,1024]{1,0:T(8,128)(2,1)S(1)} %get-tuple-element.133, s32[]{:T(128)S(6)} %select_n.90), kind=kOutput, calls=%fused_computation.7.clone.1 | convolution fusion | flops 1613757952 | bytes 4200452 | tf_op jit(solution)/shard_map/while/body/eval_jaxpr/dot_general | solution.py:72
  360.5 0.6 dynamic_slice.23
  362.7 0.5 iota_add_fusion.2
  363.2 4.0 %fusion.29 = f32[512]{0:T(512)S(1)} fusion(bf16[1536,1024]{1,0:T(8,128)(2,1)} %get-tuple-element.134, s32[512]{0:T(512)S(1)} %iota_add_fusion.2, pred[1536]{0:T(1024)(128)(4,1)S(1)} %get-tuple-element.131, bf16[1024,1024]{1,0:T(8,128)(2,1)S(1)} %get-tuple-element.133, s32[]{:T(128)S(6)} %select_n.90), kind=kOutput, calls=%fused_computation.7.clone.1 | convolution fusion | flops 1613757952 | bytes 4200452 | tf_op jit(solution)/shard_map/while/body/eval_jaxpr/dot_general | solution.py:72
  367.3 0.6 broadcast_select_fusion.1
  (22 shorter events, 0.2 us)
Async XLA Ops:
  7.2 1.8 copy-start.1
  9.0 1.6 copy-start
  18.8 287.7 %all-to-all-start = ((bf16[128,2,4,1024]{3,2,1,0:T(4,128)(2,1)}), bf16[128,2,4,1024]{3,2,1,0:T(4,128)(2,1)}, u32[]{:S(2)}, u32[]{:S(2)}) async-start(bf16[128,2,4,1024]{3,2,1,0:T(4,128)(2,1)} %reshape.106), calls=%async_computation | async-start | bytes 4194304 | tf_op jit(solution)/shard_map/all_to_all | solution.py:40
  34.8 269.8 %all-reduce.2.cloned.1.call-start = ((), (), s32[]{:S(2)}) async-start(), calls=%async_computation.2 | async-start | bytes 2097152 | tf_op jit(solution)/shard_map/psum | solution.py:50
  319.5 5.5 %copy-start.2 = (s32[1,2,256]{2,1,0:T(2,128)S(1)}, s32[1,2,256]{2,1,0:T(2,128)}, u32[]{:S(2)}) copy-start(s32[1,2,256]{2,1,0:T(2,128)} %param.7) | copy-start | bytes 6148
  335.0 14.9 %collective-permute-start = (bf16[256,1024]{1,0:T(8,128)(2,1)}, bf16[256,1024]{1,0:T(8,128)(2,1)S(1)}, u32[]{:S(2)}, u32[]{:S(2)}) collective-permute-start(bf16[256,1024]{1,0:T(8,128)(2,1)} %get-tuple-element.70), channel_id=1, source_target_pairs={{0,1},{1,2},{2,3},{3,4},{4,5},{5,6},{6,7},{7,8},{8,9},{9,10},{10,1... | collective-permute-start | bytes 1572872 | tf_op jit(solution)/shard_map/ppermute | solution.py:15
  337.1 14.7 %collective-permute-start.1 = (bf16[256,1024]{1,0:T(8,128)(2,1)}, bf16[256,1024]{1,0:T(8,128)(2,1)S(1)}, u32[]{:S(2)}, u32[]{:S(2)}) collective-permute-start(bf16[256,1024]{1,0:T(8,128)(2,1)} %get-tuple-element.71), channel_id=1, source_target_pairs={{1,0},{2,1},{3,2},{4,3},{5,4},{6,5},{7,6},{8,7},{9,8},{10,9},{11,1... | collective-permute-start | bytes 1572872 | tf_op jit(solution)/shard_map/ppermute | solution.py:15
Sparse Core Ops, SparseCore 0:
  41.0 263.4 all-reduce.1
where the time goes:
time: 376 us; the launch traced here: 375 us
  waiting for transfers between devices  275 us (73%)
  starting transfers between devices  25.7 us (7%)
  local copies, waits for them, and re-layouts  19.2 us (5%)
  other arithmetic  17.7 us (5%)
  between operations  16.3 us (4%)
  matrix products  12.1 us (3%)
  blocking collectives  5.42 us (1%)
    psum x1, waiting for transfers between devices, per_device(): total = lax.psum(partial_sums, ('dp', 'rep'))  268 us
    all_to_all x1, starting transfers between devices, per_device(): lax.all_to_all(shaped, 'dp', split_axis=0, concat_axis=0, tiled=True)  15.9 us
    ppermute x2, starting transfers between devices, from_behind(): return lax.ppermute(array, axis, pairs)  9.77 us
    dot_general x2, matrix products, one_block(): lax.dot_general(block_rows, candidates, (((1,), (1,)), ((), ())), preferr...  8.01 us
  transfers between devices with their start and end apart: 4, of which 3 were waited for; matrix products, arithmetic and copies ran while one was open for 1% of the time, Pallas kernels for 0%

commit v1 on v0

--- a/solution.py
+++ b/solution.py
@@ -34,7 +34,6 @@
     )
     unit_half = unit_full.astype(jnp.bfloat16)
     outgoing = jnp.zeros((slots, width), jnp.bfloat16).at[targets].set(unit_half)
-    member_half = member_of.astype(jnp.bfloat16)
     shaped = outgoing.reshape(n_chips, n_cores, capacity, width)
     arrived = lax.all_to_all(
         lax.all_to_all(shaped, "dp", split_axis=0, concat_axis=0, tiled=True),
@@ -44,11 +43,9 @@
         tiled=True,
     )
     members = arrived.reshape(slots, width)
-    partial_sums = lax.dot_general(
-        member_half, unit_half, (((0,), (0,)), ((), ())), preferred_element_type=jnp.float32
+    own_sum = lax.dot_general(
+        jnp.ones((1, slots), jnp.bfloat16), members, (((1,), (0,)), ((), ())), preferred_element_type=jnp.float32
     )
-    total = lax.psum(partial_sums, ("dp", "rep"))
-    own_sum = lax.dynamic_slice_in_dim(total, me, 1, 0)
     direction = own_sum[0] * lax.rsqrt(jnp.sum(own_sum * own_sum) + eps)
     lengths = jnp.einsum("se,se->s", members, members, preferred_element_type=jnp.float32)
     filled = lengths > 0.5

time: 376 us -> 138 us (0.37)
  waiting for transfers between devices: 275 us -> 6.91 us
  blocking collectives: 5.42 us -> 72.6 us
  starting transfers between devices: 25.7 us -> 9.77 us
  between operations: 16.3 us -> 2.89 us
    psum x1 -> x0, waiting for transfers between devices: 268 us -> none  [per_device(): total = lax.psum(partial_sums, ('dp', 'rep'))]
    all_to_all x0 -> x1, blocking collectives: none -> 67.1 us  [per_device(): lax.all_to_all(shaped, 'dp', split_axis=0, concat_axis=0, tiled=True)]
    all_to_all x1 -> x0, starting transfers between devices: 15.9 us -> none  [per_device(): lax.all_to_all(shaped, 'dp', split_axis=0, concat_axis=0, tiled=True)]
  transfers between devices with their start and end apart: 4 -> 2, of which waited for: 3 -> 2; matrix products, arithmetic and copies ran while one was open for 1% -> 0% of each run, Pallas kernels for 0% -> 0%
where the time goes in v1:
time: 138 us; the launch traced here: 137 us
  blocking collectives  72.6 us (53%)
  local copies, waits for them, and re-layouts  16.3 us (12%)
  other arithmetic  15.4 us (11%)
  matrix products  10.1 us (7%)
  starting transfers between devices  9.77 us (7%)
  waiting for transfers between devices  6.91 us (5%)
  loops' own time  3.3 us (2%)
  between operations  2.89 us (2%)
    all_to_all x1, blocking collectives, per_device(): lax.all_to_all(shaped, 'dp', split_axis=0, concat_axis=0, tiled=True)  67.1 us
    ppermute x2, starting transfers between devices, from_behind(): return lax.ppermute(array, axis, pairs)  9.77 us
    dot_general x2, matrix products, one_block(): lax.dot_general(block_rows, candidates, (((1,), (1,)), ((), ())), preferr...  8.01 us
    ppermute x2, waiting for transfers between devices, from_behind(): return lax.ppermute(array, axis, pairs)  6.91 us
    all_to_all x1, blocking collectives, per_device(): lax.all_to_all(lax.all_to_all(shaped, 'dp', split_axis=0, concat_axis=0,...  5.42 us
    sort x1, other arithmetic, per_device(): order = jnp.argsort(1 - filled_int, stable=True)  4.37 us
    scatter x1, other arithmetic, per_device(): jnp.zeros((slots, width), jnp.bfloat16).at[targets].set(unit_half)  4.22 us
    another operation x1, loops' own time, per_device(): best = lax.map(one_block, starts).reshape(slots)  3.3 us
  transfers between devices with their start and end apart: 2, of which 2 were waited for; matrix products, arithmetic and copies ran while one was open for 0% of the time, Pallas kernels for 0%

profile of v1, /device:TPU:8, one launch (start us, length us, event | category | flops | bytes accessed | tf_op | source)
XLA Modules:
  0.0 137.2 jit_solution(18101900111716776001)
XLA Ops:
  0.6 0.0 copy-start.1
  0.6 0.0 copy-start
  0.6 0.9 copy.12
  1.6 0.2 fusion.11
  1.9 0.1 copy.13
  2.0 0.0 copy-done.1
  2.0 0.2 fusion.10
  2.3 0.0 copy-done
  2.3 0.2 multiply_reduce_fusion
  2.5 4.2 %scatter_custom_fusion = bf16[1024,1024]{1,0:T(8,128)(2,1)} fusion(s32[512]{0:T(512)S(1)} %bitcast.60, f32[512,1024]{1,0:T(8,128)S(1)} %copy-done, f32[512]{0:T(512)S(1)} %add_rsqrt_fusion, bf16[]{:T(256)} %constant.27.clone.1), kind=kCustom, calls=%fused_computation.16 | custom fusion | flops 1048576 | bytes 4196354 | tf_op jit(solution)/shard_map/scatter | solution.py:36
  6.7 2.7 %reshape.111 = bf16[128,2,4,1024]{3,2,1,0:T(4,128)(2,1)S(1)} reshape(bf16[1024,1024]{1,0:T(8,128)(2,1)} %scatter_custom_fusion) | data formatting | bytes 4194304 | tf_op jit(solution)/shard_map/reshape | solution.py:37
  9.5 67.1 %all_to_all.10 = bf16[128,2,4,1024]{3,2,1,0:T(4,128)(2,1)S(1)} all-to-all(bf16[128,2,4,1024]{3,2,1,0:T(4,128)(2,1)S(1)} %reshape.111), channel_id=1, replica_groups=mesh['dp'=128,'rep'=2] {'dp'}, dimensions={0} | all-to-all | bytes 4194304 | tf_op jit(solution)/shard_map/all_to_all | solution.py:39
  76.6 0.7 copy.14
  77.3 5.4 %all_to_all.11 = bf16[128,2,4,1024]{3,2,0,1:T(4,128)(2,1)S(1)} all-to-all(bf16[128,2,4,1024]{3,2,0,1:T(4,128)(2,1)S(1)} %copy.14), channel_id=1, replica_groups=mesh['dp'=128,'rep'=2] {'rep'}, dimensions={1} | all-to-all | bytes 4194304 | tf_op jit(solution)/shard_map/all_to_all | solution.py:38
  82.8 2.6 %copy.15 = bf16[128,2,4,1024]{3,2,1,0:T(4,128)(2,1)} copy(bf16[128,2,4,1024]{3,2,0,1:T(4,128)(2,1)S(1)} %all_to_all.11) | data formatting | bytes 4194304 | tf_op jit(solution)/shard_map/all_to_all | solution.py:38
  85.4 2.5 %reshape.112 = bf16[1024,1024]{1,0:T(8,128)(2,1)S(1)} reshape(bf16[128,2,4,1024]{3,2,1,0:T(4,128)(2,1)} %copy.15) | data formatting | bytes 4194304 | tf_op jit(solution)/shard_map/reshape | solution.py:45
  87.9 0.4 fusion.14
  88.3 0.0 copy-start.2
  88.3 0.5 fusion.6
  88.8 0.6 multiply_reduce_fusion.1
  90.1 1.7 %fusion.18 = f32[1,1024]{1,0:T(1,128)S(1)} fusion(bf16[1024,1024]{1,0:T(8,128)(2,1)S(1)} %reshape.112, f32[1024,1]{0,1:T(1,128)S(1)} %bitcast.50), kind=kOutput, calls=%fused_computation.50 | convolution fusion | flops 12582912 | bytes 2105344 | tf_op jit(solution)/shard_map/dot_general | solution.py:79
  91.8 0.6 broadcast_select_fusion
  92.4 0.6 convert_reduce_fusion
  94.4 0.0 copy-done.2
  94.4 0.1 remainder_bitcast_fusion
  94.6 4.4 %sort.17 = (s32[1024]{0:T(1024)}, s32[1024]{0:T(1024)S(1)}) sort(s32[1024]{0:T(1024)S(1)} %get-tuple-element.73, s32[1024]{0:T(1024)S(1)} %iota.25), dimensions={0}, to_apply=%region_5.6 | sort | flops 10240 | bytes 16384 | tf_op jit(solution)/shard_map/jit(argsort)/sort | solution.py:54
  98.9 2.3 %gather_fusion = s32[512]{0:T(512)S(1)} fusion(s32[1024]{0:T(1024)S(1)} %get-tuple-element.40, s32[1024]{0:T(1024)S(1)} %pad_clamp_fusion.1), kind=kCustom, calls=%fused_computation | custom fusion | bytes 6144 | tf_op jit(solution)/shard_map/gather | solution.py:56
  101.2 2.1 %gather_fusion.1 = bf16[512,1024]{1,0:T(8,128)(2,1)S(1)} fusion(bf16[1024,1024]{1,0:T(8,128)(2,1)S(1)} %reshape.112, s32[1024]{0:T(1024)S(1)} %pad_clamp_fusion), kind=kCustom, calls=%fused_computation.1 | custom fusion | bytes 2099200 | tf_op jit(solution)/shard_map/gather | solution.py:57
  103.3 1.1 fusion.17
  104.4 2.0 %collective-permute-start = (bf16[256,1024]{1,0:T(8,128)(2,1)}, bf16[256,1024]{1,0:T(8,128)(2,1)S(1)}, u32[]{:S(2)}, u32[]{:S(2)}) collective-permute-start(bf16[256,1024]{1,0:T(8,128)(2,1)} %get-tuple-element.70), channel_id=1, source_target_pairs={{0,1},{1,2},{2,3},{3,4},{4,5},{5,6},{6,7},{7,8},{8,9},{9,10},{10,1... | collective-permute-start | bytes 1572872 | tf_op jit(solution)/shard_map/ppermute | solution.py:15
  106.4 7.7 %collective-permute-start.1 = (bf16[256,1024]{1,0:T(8,128)(2,1)}, bf16[256,1024]{1,0:T(8,128)(2,1)S(1)}, u32[]{:S(2)}, u32[]{:S(2)}) collective-permute-start(bf16[256,1024]{1,0:T(8,128)(2,1)} %get-tuple-element.71), channel_id=1, source_target_pairs={{1,0},{2,1},{3,2},{4,3},{5,4},{6,5},{7,6},{8,7},{9,8},{10,9},{11,1... | collective-permute-start | bytes 1572872 | tf_op jit(solution)/shard_map/ppermute | solution.py:15
  114.2 5.1 %collective-permute-done = bf16[256,1024]{1,0:T(8,128)(2,1)S(1)} collective-permute-done((bf16[256,1024]{1,0:T(8,128)(2,1)}, bf16[256,1024]{1,0:T(8,128)(2,1)S(1)}, u32[]{:S(2)}, u32[]{:S(2)}) %collective-permute-start) | collective-permute-done | bytes 524320 | tf_op jit(solution)/shard_map/ppermute | solution.py:15
  119.3 1.9 %collective-permute-done.1 = bf16[256,1024]{1,0:T(8,128)(2,1)S(1)} collective-permute-done((bf16[256,1024]{1,0:T(8,128)(2,1)}, bf16[256,1024]{1,0:T(8,128)(2,1)S(1)}, u32[]{:S(2)}, u32[]{:S(2)}) %collective-permute-start.1) | collective-permute-done | bytes 524320 | tf_op jit(solution)/shard_map/ppermute | solution.py:15
  121.1 1.9 %pad_maximum_fusion = bf16[1536,1024]{1,0:T(8,128)(2,1)} fusion(bf16[256,1024]{1,0:T(8,128)(2,1)S(1)} %collective-permute-done.1, bf16[256,1024]{1,0:T(8,128)(2,1)S(1)} %collective-permute-done, bf16[1024,1024]{1,0:T(8,128)(2,1)S(1)} %reshape.112), kind=kLoop, calls=%fused_computation.13 | loop fusion | flops 9437184 | bytes 6291456 | tf_op jit(solution)/shard_map/concatenate | solution.py:60
  123.0 13.6 %while.11 = (s32[]{:T(128)}, f32[2,512]{1,0:T(2,128)S(1)}, pred[1536]{0:T(1024)(128)(4,1)S(1)}, s32[2]{0:T(128)S(1)}, bf16[1024,1024]{1,0:T(8,128)(2,1)S(1)}, /*...) while((s32[]{:T(128)}, f32[2,512]{1,0:T(2,128)S(1)}, ...), condition=%wide.region_9.10_spmd.clone, body=%wide.region_7.9_spmd.clone.sunk | while | flops 1613758464 | bytes 4206743 | solution.py:77
  123.0 0.5 dynamic_slice.14
  125.2 0.5 iota_add_fusion.2
  125.8 4.0 %fusion.28 = f32[512]{0:T(512)S(1)} fusion(bf16[1536,1024]{1,0:T(8,128)(2,1)} %get-tuple-element.134, s32[512]{0:T(512)S(1)} %iota_add_fusion.2, pred[1536]{0:T(1024)(128)(4,1)S(1)} %get-tuple-element.131, bf16[1024,1024]{1,0:T(8,128)(2,1)S(1)} %get-tuple-element.133, s32[]{:T(128)S(6)} %select_n.86), kind=kOutput, calls=%fused_computation.7.clone.1 | convolution fusion | flops 1613757952 | bytes 4200452 | tf_op jit(solution)/shard_map/while/body/eval_jaxpr/dot_general | solution.py:69
  129.8 0.6 dynamic_slice.14
  132.0 0.5 iota_add_fusion.2
  132.6 4.0 %fusion.28 = f32[512]{0:T(512)S(1)} fusion(bf16[1536,1024]{1,0:T(8,128)(2,1)} %get-tuple-element.134, s32[512]{0:T(512)S(1)} %iota_add_fusion.2, pred[1536]{0:T(1024)(128)(4,1)S(1)} %get-tuple-element.131, bf16[1024,1024]{1,0:T(8,128)(2,1)S(1)} %get-tuple-element.133, s32[]{:T(128)S(6)} %select_n.86), kind=kOutput, calls=%fused_computation.7.clone.1 | convolution fusion | flops 1613757952 | bytes 4200452 | tf_op jit(solution)/shard_map/while/body/eval_jaxpr/dot_general | solution.py:69
  136.7 0.6 broadcast_select_fusion.1
  (23 shorter events, 0.3 us)
Async XLA Ops:
  0.6 1.4 %copy-start.1 = (s32[512,1]{0,1:T(1,128)S(1)}, s32[512,1]{0,1:T(1,128)}, u32[]{:S(2)}) copy-start(s32[512,1]{0,1:T(1,128)} %param.6) | copy-start | bytes 6148
  0.6 1.6 %copy-start = (f32[512,1024]{1,0:T(8,128)S(1)}, f32[512,1024]{1,0:T(8,128)}, u32[]{:S(2)}) copy-start(f32[512,1024]{1,0:T(8,128)} %param.5) | copy-start | bytes 6291460
  88.3 6.1 %copy-start.2 = (s32[1,2,256]{2,1,0:T(2,128)S(1)}, s32[1,2,256]{2,1,0:T(2,128)}, u32[]{:S(2)}) copy-start(s32[1,2,256]{2,1,0:T(2,128)} %param.7) | copy-start | bytes 6148
  104.4 14.9 %collective-permute-start = (bf16[256,1024]{1,0:T(8,128)(2,1)}, bf16[256,1024]{1,0:T(8,128)(2,1)S(1)}, u32[]{:S(2)}, u32[]{:S(2)}) collective-permute-start(bf16[256,1024]{1,0:T(8,128)(2,1)} %get-tuple-element.70), channel_id=1, source_target_pairs={{0,1},{1,2},{2,3},{3,4},{4,5},{5,6},{6,7},{7,8},{8,9},{9,10},{10,1... | collective-permute-start | bytes 1572872 | tf_op jit(solution)/shard_map/ppermute | solution.py:15
  106.4 14.7 %collective-permute-start.1 = (bf16[256,1024]{1,0:T(8,128)(2,1)}, bf16[256,1024]{1,0:T(8,128)(2,1)S(1)}, u32[]{:S(2)}, u32[]{:S(2)}) collective-permute-start(bf16[256,1024]{1,0:T(8,128)(2,1)} %get-tuple-element.71), channel_id=1, source_target_pairs={{1,0},{2,1},{3,2},{4,3},{5,4},{6,5},{7,6},{8,7},{9,8},{10,9},{11,1... | collective-permute-start | bytes 1572872 | tf_op jit(solution)/shard_map/ppermute | solution.py:15

commit v2 on v1

v2 whole, which is shorter than its diff:
```python
import functools

import jax
import jax.numpy as jnp
from jax import lax
from jax.experimental import pallas as pl
from jax.experimental.pallas import tpu as pltpu
from jax.sharding import PartitionSpec as P

MESH = pl.DeviceIdType.MESH
SLOTS = 1024
CAP = 4
Y, Z, X, C = 4, 8, 4, 2
DEVICES = Y * Z * X * C
SIDE = 16
EPS = 1e-06
MARK = 2.0
F32 = jnp.float32
BF16 = jnp.bfloat16


def iota(shape, dim):
    return lax.broadcasted_iota(jnp.int32, shape, dim)


def rows_dot(a, b):
    return lax.dot_general(a, b, (((1,), (1,)), ((), ())), preferred_element_type=F32)


def device(flat):
    return (flat // C, lax.rem(flat, C))


def kernel(
    emb_ref, lab_ref, bnd_ref, best_ref, cent_ref,
    out_buf, in_buf, members, picks, outward, lower, upper,
    stage_sem, send_sem, recv_sem, own_sem, side_send, side_recv,
):
    rows, width = emb_ref.shape
    bound = bnd_ref.shape[1]
    dp, core = lax.axis_index("dp"), lax.axis_index("rep")
    me = dp * C + core
    my_y, my_z, my_x = dp // (Z * X), lax.rem(dp // X, Z), lax.rem(dp, X)
    hi, lo = me // SIDE, lax.rem(me, SIDE)

    def row_mate(i):
        return hi * SIDE + lax.rem(lo + i, SIDE)

    def column_mate(i):
        return lax.rem(hi + i, SIDE) * SIDE + lo

    barrier = pltpu.get_barrier_semaphore()

    def greet(i, _):
        pl.semaphore_signal(barrier, inc=1, device_id=device(row_mate(i)), device_id_type=MESH)
        pl.semaphore_signal(barrier, inc=1, device_id=device(column_mate(i)), device_id_type=MESH)
        return 0

    lax.fori_loop(1, SIDE, greet, 0)

    lab = lab_ref[...].astype(F32)
    lab_col = jnp.broadcast_to(lab, (128, rows)).T
    lab_col = jnp.concatenate([lab_col] * (rows // 128), axis=1)
    earlier = (lab_col == lab) & (iota((rows, rows), 0) < iota((rows, rows), 1))
    rank = jnp.sum(jnp.where(earlier, 1.0, 0.0), axis=0, keepdims=True)
    target = lab * CAP + rank

    emb = emb_ref[...]
    unit = (emb * lax.rsqrt(jnp.sum(emb * emb, axis=1, keepdims=True) + EPS)).astype(BF16)

    pl.semaphore_wait(barrier, 2 * (SIDE - 1))

    def second(i, _):
        pl.semaphore_signal(stage_sem, inc=1, device_id=device(row_mate(i)), device_id_type=MESH)
        return 0

    lax.fori_loop(1, SIDE, second, 0)

    step = 128

    def build(i, _):
        slot = (iota((step, rows), 0) + i * step).astype(F32)
        chosen = slot == target
        some = jnp.sum(jnp.where(chosen, 1.0, 0.0), axis=1, keepdims=True)
        block = jnp.dot(jnp.where(chosen, 1.0, 0.0).astype(BF16), unit, preferred_element_type=F32)
        empty = (some < 0.5) & (iota((step, width), 1) == 0)
        block = jnp.where(empty, MARK, block)
        out_buf[pl.ds(i * (step // CAP), step // CAP)] = block.astype(BF16).reshape(step // CAP, CAP, width)
        return 0

    lax.fori_loop(0, SLOTS // step, build, 0)

    pl.semaphore_wait(stage_sem, SIDE - 1)

    plane = Y * X * C

    def send_to(dy, dz, dx, dc):
        t = (lax.rem(my_y + dy, Y) * Z + lax.rem(my_z + dz, Z)) * X + lax.rem(my_x + dx, X)
        c = lax.rem(core + dc, C)
        pltpu.make_async_remote_copy(
            out_buf.at[t * C + c], in_buf.at[me], send_sem, recv_sem.at[dz],
            device_id=(t, c), device_id_type=MESH,
        ).start()

    own = pltpu.make_async_copy(out_buf.at[me], in_buf.at[me], own_sem)
    own.start()
    for dz in (4, 3, 5, 2, 6, 1, 7, 0):
        def one(i, _, dz=dz):
            send_to(i // (X * C), dz, lax.rem(i // C, X), lax.rem(i, C))
            return 0

        lax.fori_loop(1 if dz == 0 else 0, plane, one, 0)

    raw = bnd_ref[...].astype(F32)
    for side in range(2):
        picks[pl.ds(side * bound, bound)] = jnp.broadcast_to(raw[side : side + 1], (128, bound)).T

    own.wait()
    for dz in (4, 3, 5, 2, 6, 1, 7, 0):
        n = plane - 1 if dz == 0 else plane
        pltpu.make_async_remote_copy(
            in_buf.at[pl.ds(0, n)], in_buf.at[pl.ds(0, n)], send_sem, recv_sem.at[dz],
            device_id=device(row_mate(1)), device_id_type=MESH,
        ).wait_recv()
        z = lax.rem(my_z + Z - dz, Z)
        for y in range(Y):
            first = y * (Z * X * C) + z * (X * C)
            members[pl.ds(pl.multiple_of(first * CAP, X * C * CAP), X * C * CAP)] = in_buf[
                pl.ds(first, X * C)
            ].reshape(X * C * CAP, width)

    corner = jnp.where(iota((8, 128), 1) == 0, 1.0, 0.0).astype(BF16)
    heads = rows_dot(corner, members[:, :128])[:1]
    filled = jnp.where(heads < 1.5, 1.0, 0.0)
    groups = SLOTS // 128
    stacked = jnp.concatenate([filled[:, k * 128 : (k + 1) * 128] for k in range(groups)], axis=0)
    upto = jnp.where(iota((128, 128), 0) <= iota((128, 128), 1), 1.0, 0.0).astype(BF16)
    within = jnp.dot(stacked.astype(BF16), upto, preferred_element_type=F32)
    totals = jnp.sum(stacked, axis=1, keepdims=True)
    count = jnp.sum(totals, axis=0, keepdims=True)
    order = []
    before = jnp.zeros((1, 1), F32)
    for k in range(groups):
        order.append(jnp.where(stacked[k : k + 1] > 0.5, within[k : k + 1] + (before - 1.0), -1.0))
        before = before + totals[k : k + 1]

    def choose(first, size):
        want = picks[pl.ds(first, size)]
        want = want - jnp.floor((want + 0.5) / count) * count
        return jnp.concatenate([jnp.where(want == order[k], 1.0, 0.0).astype(BF16) for k in range(groups)], axis=1)

    table = members[...]
    for side in range(2):
        outward[pl.ds(side * bound, bound)] = jnp.dot(
            choose(side * bound, bound), table, preferred_element_type=F32
        ).astype(BF16)
    above, below = lax.rem(me + 1, DEVICES), lax.rem(me + DEVICES - 1, DEVICES)
    up = pltpu.make_async_remote_copy(
        outward.at[pl.ds(bound, bound)], lower, side_send.at[0], side_recv.at[0],
        device_id=device(above), device_id_type=MESH,
    )
    down = pltpu.make_async_remote_copy(
        outward.at[pl.ds(0, bound)], upper, side_send.at[1], side_recv.at[1],
        device_id=device(below), device_id_type=MESH,
    )
    up.start()
    down.start()

    weights = jnp.broadcast_to(filled, (8, SLOTS)).astype(BF16)
    sums = jnp.dot(weights, table, preferred_element_type=F32)[:1]
    direction = sums * lax.rsqrt(jnp.sum(sums * sums, axis=1, keepdims=True) + EPS)
    high = direction.astype(BF16)
    rest = direction - high.astype(F32)
    middle = rest.astype(BF16)
    low = (rest - middle.astype(F32)).astype(BF16)
    row = iota((8, width), 0)
    parts = jnp.where(row == 0, high.astype(F32), jnp.where(row == 1, middle.astype(F32), jnp.where(row == 2, low.astype(F32), 0.0)))
    central = jnp.sum(rows_dot(parts.astype(BF16), table), axis=0, keepdims=True)
    cent_ref[...] = jnp.where(filled > 0.5, central, 0.0)

    chunk = 256
    best = jnp.full((8, SLOTS), -1.0, F32)
    for first in range(0, SLOTS, chunk):
        scores = rows_dot(members[first : first + chunk], table)
        empty = members[first : first + chunk, :128][:, :1].astype(F32) > 1.5
        barred = empty | (iota((chunk, SLOTS), 0) + first == iota((chunk, SLOTS), 1))
        scores = jnp.where(barred, -1.0, scores)
        best = jnp.maximum(best, jnp.max(scores.reshape(chunk // 8, 8, SLOTS), axis=0))

    up.wait()
    down.wait()
    for buf, there in ((lower, me > 0), (upper, me < DEVICES - 1)):
        scores = rows_dot(buf[...], table)
        top = jnp.max(scores.reshape(bound // 8, 8, SLOTS), axis=0)
        best = jnp.maximum(best, jnp.where(there, top, -1.0))
    nearest = jnp.max(best, axis=0, keepdims=True)
    best_ref[...] = jnp.where(filled > 0.5, nearest, 0.0)

    n = DEVICES - 1
    pltpu.make_async_remote_copy(
        out_buf.at[pl.ds(0, n)], out_buf.at[pl.ds(0, n)], send_sem, recv_sem.at[0],
        device_id=device(row_mate(1)), device_id_type=MESH,
    ).wait_send()


def per_device(embeddings, cluster_ids, boundary_slots):
    rows, width = embeddings.shape
    bound = boundary_slots.shape[2]
    vmem = pl.BlockSpec(memory_space=pltpu.VMEM)
    return pl.pallas_call(
        kernel,
        out_shape=(jax.ShapeDtypeStruct((1, SLOTS), F32), jax.ShapeDtypeStruct((1, SLOTS), F32)),
        in_specs=[vmem, vmem, vmem],
        out_specs=(vmem, vmem),
        scratch_shapes=[
            pltpu.VMEM((DEVICES, CAP, width), BF16),
            pltpu.VMEM((DEVICES, CAP, width), BF16),
            pltpu.VMEM((SLOTS, width), BF16),
            pltpu.VMEM((2 * bound, 128), F32),
            pltpu.VMEM((2 * bound, width), BF16),
            pltpu.VMEM((bound, width), BF16),
            pltpu.VMEM((bound, width), BF16),
            pltpu.SemaphoreType.REGULAR,
            pltpu.SemaphoreType.DMA,
            pltpu.SemaphoreType.DMA((Z,)),
            pltpu.SemaphoreType.DMA,
            pltpu.SemaphoreType.DMA((2,)),
            pltpu.SemaphoreType.DMA((2,)),
        ],
        compiler_params=pltpu.CompilerParams(collective_id=0, has_side_effects=True, vmem_limit_bytes=48 << 20),
    )(embeddings, cluster_ids.reshape(1, rows), boundary_slots[0])


def solution(mesh):
    placed = (P(("dp", "rep"), None), P(("dp", "rep"), None), P(("dp", "rep"), None, None))
    return jax.shard_map(
        per_device,
        mesh=mesh,
        in_specs=placed,
        out_specs=(P(("dp", "rep"), None), P(("dp", "rep"), None)),
        check_vma=False,
    )
```

time: 138 us -> 80.1 us (0.58)
  Pallas kernels: 0 us -> 74.6 us
  blocking collectives: 72.6 us -> 0 us
  other arithmetic: 15.4 us -> 0 us
  local copies, waits for them, and re-layouts: 16.3 us -> 4.13 us
  matrix products: 10.1 us -> 0 us
  starting transfers between devices: 9.77 us -> 0 us
  waiting for transfers between devices: 6.91 us -> 0 us
  loops' own time: 3.3 us -> 0 us
  between operations: 2.89 us -> 0.65 us
    pallas_call x0 -> x1, Pallas kernels: none -> 74.6 us  [per_device(): pl.pallas_call(kernel, out_shape=(jax.ShapeDtypeStruct((1, SLOTS), F32),...]
    all_to_all x2 -> x0, blocking collectives: 72.6 us -> none  [the longest x1 67.1 us: per_device(): lax.all_to_all(shaped, 'dp', split_axis=0, concat_axis=0, tiled=True)]
    dot_general x4 -> x0, matrix products: 10.1 us -> none  [the longest x2 8.01 us: one_block(): lax.dot_general(block_rows, candidates, (((1,), (1,)), ((), ())), preferr...]
    ppermute x2 -> x0, starting transfers between devices: 9.77 us -> none  [from_behind(): return lax.ppermute(array, axis, pairs)]
    ppermute x2 -> x0, waiting for transfers between devices: 6.91 us -> none  [from_behind(): return lax.ppermute(array, axis, pairs)]
    reshape x2 -> x0, local copies, waits for them, and re-layouts: 5.27 us -> none  [the longest x1 2.73 us: per_device(): shaped = outgoing.reshape(n_chips, n_cores, capacity, width)]
    sort x1 -> x0, other arithmetic: 4.37 us -> none  [per_device(): order = jnp.argsort(1 - filled_int, stable=True)]
    gather x2 -> x0, local copies, waits for them, and re-layouts: 4.34 us -> none  [the longest x1 2.28 us: per_device(): positions = order[picks.reshape(-1)]]
  transfers between devices with their start and end apart: 2 -> 0, of which waited for: 2 -> 0; matrix products, arithmetic and copies ran while one was open for 0% -> 0% of each run, Pallas kernels for 0% -> 0%
where the time goes in v2:
time: 80.1 us; the launch traced here: 79.4 us
  Pallas kernels  74.6 us (93%)
  local copies, waits for them, and re-layouts  4.13 us (5%)
    pallas_call x1, Pallas kernels, per_device(): pl.pallas_call(kernel, out_shape=(jax.ShapeDtypeStruct((1, SLOTS), F32),...  74.6 us
    unnamed x8, local copies, waits for them, and re-layouts  4.13 us

profile of v2, /device:TPU:8, one launch (start us, length us, event | category | flops | bytes accessed | tf_op | source)
XLA Modules:
  0.0 79.4 jit_solution(4847758280574052341)
XLA Ops:
  0.6 0.0 copy-start
  0.6 1.6 %copy-done = f32[512,1024]{1,0:T(8,128)S(1)} copy-done((f32[512,1024]{1,0:T(8,128)S(1)}, f32[512,1024]{1,0:T(8,128)}, u32[]{:S(2)}) %copy-start) | copy-done | bytes 2097176
  2.2 0.0 copy-start.1
  2.2 0.7 copy-done.1
  2.9 0.0 copy-start.2
  2.9 0.7 copy-done.2
  3.6 74.6 %shard_map.50 = (f32[1,1024]{1,0:T(1,128)S(1)}, f32[1,1024]{1,0:T(1,128)S(1)}) custom-call(f32[512,1024]{1,0:T(8,128)S(1)} %copy-done, s32[1,512]{1,0:T(1,128)S(1)} %bitcast.2, s32[2,256]{1,0:T(2,128)S(1)} %bitcast.3), custom_call_target="tpu_custom_call" | custom-call | tf_op jit(solution)/shard_map/pallas_call | solution.py:210
  78.2 0.6 copy.7
  78.8 0.6 copy.8
Async XLA Ops:
  0.6 1.6 %copy-start = (f32[512,1024]{1,0:T(8,128)S(1)}, f32[512,1024]{1,0:T(8,128)}, u32[]{:S(2)}) copy-start(f32[512,1024]{1,0:T(8,128)} %emb_ref.1) | copy-start | bytes 6291460
  2.2 0.7 copy-start.1
  2.9 0.7 copy-start.2

commit v3 on v1

v3 whole, which is shorter than its diff:
```python
import functools

import jax
import jax.numpy as jnp
from jax import lax
from jax.experimental import pallas as pl
from jax.experimental.pallas import tpu as pltpu
from jax.sharding import PartitionSpec as P

MESH = pl.DeviceIdType.MESH
SLOTS = 1024
CAP = 4
DIRECT = 2
HOPPED = CAP - DIRECT
SPILL = 16
Y, Z, X, C = 4, 8, 4, 2
XC = X * C
PLANE = Y * XC
DEVICES = Z * PLANE
SIDE = 16
LANES = 128
EPS = 1e-06
EMPTY = 2.0
FULL = 8.0
ORDER = (4, 3, 5, 2, 6, 1, 7, 0)
F32 = jnp.float32
BF16 = jnp.bfloat16


def iota(shape, dim):
    return lax.broadcasted_iota(jnp.int32, shape, dim)


def rows_dot(a, b):
    return lax.dot_general(a, b, (((1,), (1,)), ((), ())), preferred_element_type=F32)


def device(flat):
    return (flat // C, lax.rem(flat, C))


def along_sublanes(row, size):
    turned = jnp.broadcast_to(row, (LANES, row.shape[1])).T
    return jnp.concatenate([turned] * (size // LANES), axis=1)


def earlier_equal(key, size):
    same = (along_sublanes(key, size) == key) & (iota((size, size), 0) < iota((size, size), 1))
    return jnp.sum(jnp.where(same, 1.0, 0.0), axis=0, keepdims=True)


def place():
    dp, core = lax.axis_index("dp"), lax.axis_index("rep")
    return dp * C + core, dp // (Z * X), lax.rem(dp // X, Z), lax.rem(dp, X), core


def row_mate(me, i):
    return me // SIDE * SIDE + lax.rem(me + i, SIDE)


def column_mate(me, i):
    return lax.rem(me // SIDE + i, SIDE) * SIDE + lax.rem(me, SIDE)


def greet(me):
    barrier = pltpu.get_barrier_semaphore()

    def one(i, _):
        pl.semaphore_signal(barrier, inc=1, device_id=device(row_mate(me, i)), device_id_type=MESH)
        pl.semaphore_signal(barrier, inc=1, device_id=device(column_mate(me, i)), device_id_type=MESH)
        return 0

    lax.fori_loop(1, SIDE, one, 0)


def pass_on(me, stage_sem):
    pl.semaphore_wait(pltpu.get_barrier_semaphore(), 2 * (SIDE - 1))

    def one(i, _):
        pl.semaphore_signal(stage_sem, inc=1, device_id=device(row_mate(me, i)), device_id_type=MESH)
        return 0

    lax.fori_loop(1, SIDE, one, 0)


def fetch(sources, targets, sems):
    copies = [pltpu.make_async_copy(s, t, sems.at[k]) for k, (s, t) in enumerate(zip(sources, targets))]
    for copy in copies:
        copy.start()
    return copies


def normalise(emb_ref, unit):
    rows = emb_ref.shape[0]
    step = 128

    def one(i, _):
        at = pl.ds(pl.multiple_of(i * step, step), step)
        emb = emb_ref[at, :]
        unit[at, :] = (emb * lax.rsqrt(jnp.sum(emb * emb, axis=1, keepdims=True) + EPS)).astype(BF16)
        return 0

    lax.fori_loop(0, rows // step, one, 0)


def build(target, unit, buf, total, per, full=None):
    rows, width = unit.shape
    step = 128

    def one(i, _):
        slot = (iota((step, rows), 0) + i * step).astype(F32)
        chosen = jnp.where(slot == target, 1.0, 0.0)
        some = jnp.sum(chosen, axis=1, keepdims=True)
        block = jnp.dot(chosen.astype(BF16), unit[...], preferred_element_type=F32)
        first = iota((step, width), 1) == 0
        block = jnp.where((some < 0.5) & first, EMPTY, block)
        if full is not None:
            block = jnp.where((full > 0.5) & first, FULL, block)
        buf[pl.ds(i * (step // per), step // per)] = block.astype(BF16).reshape(step // per, per, width)
        return 0

    lax.fori_loop(0, total // step, one, 0)


def turn_picks(bnd_ref, picks):
    bound = bnd_ref.shape[1]
    raw = bnd_ref[...].astype(F32)
    for side in range(2):
        picks[pl.ds(side * bound, bound)] = jnp.broadcast_to(raw[side : side + 1], (LANES, bound)).T


def send_group(place_of_me, dz, source, target, send_sem, recv_sem):
    me, my_y, my_z, my_x, core = place_of_me

    def one(i, _):
        t = (lax.rem(my_y + i // XC, Y) * Z + lax.rem(my_z + dz, Z)) * X + lax.rem(my_x + i // C, X)
        c = lax.rem(core + i, C)
        pltpu.make_async_remote_copy(
            source.at[t * C + c], target.at[me], send_sem, recv_sem.at[dz],
            device_id=(t, c), device_id_type=MESH,
        ).start()
        return 0

    lax.fori_loop(1 if dz == 0 else 0, PLANE, one, 0)


def awaited(me, ref, n, send_sem, recv_sem):
    view = ref.at[pl.ds(0, n)]
    return pltpu.make_async_remote_copy(
        view, view, send_sem, recv_sem, device_id=device(row_mate(me, 1)), device_id_type=MESH
    )


def finish(me, members, picks, outward, beside, side_send, side_recv, best_ref, cent_ref):
    width = members.shape[1]
    bound = outward.shape[0] // 2
    groups = SLOTS // LANES

    corner = jnp.where(iota((8, LANES), 1) == 0, 1.0, 0.0).astype(BF16)
    heads = rows_dot(corner, members[:, :LANES])[:1]
    filled = jnp.where(heads < 1.5, 1.0, 0.0)
    stacked = jnp.concatenate([filled[:, k * LANES : (k + 1) * LANES] for k in range(groups)], axis=0)
    upto = jnp.where(iota((LANES, LANES), 0) <= iota((LANES, LANES), 1), 1.0, 0.0).astype(BF16)
    within = jnp.dot(stacked.astype(BF16), upto, preferred_element_type=F32)
    totals = jnp.sum(stacked, axis=1, keepdims=True)
    count = jnp.sum(totals, axis=0, keepdims=True)
    order = []
    before = jnp.zeros((1, 1), F32)
    for k in range(groups):
        order.append(jnp.where(stacked[k : k + 1] > 0.5, within[k : k + 1] + (before - 1.0), -1.0))
        before = before + totals[k : k + 1]

    half = bound // 2
    above, below = lax.rem(me + 1, DEVICES), lax.rem(me + DEVICES - 1, DEVICES)
    table = members[...]
    copies = []
    for part in range(2):
        for side, peer in ((1, above), (0, below)):
            at = pl.ds(side * bound + part * half, half)
            want = picks[at]
            want = want - jnp.floor((want + 0.5) / count) * count
            chosen = [jnp.where(want == order[k], 1.0, 0.0).astype(BF16) for k in range(groups)]
            outward[at] = jnp.dot(jnp.concatenate(chosen, axis=1), table, preferred_element_type=F32).astype(BF16)
            copy = pltpu.make_async_remote_copy(
                outward.at[at], beside.at[at], side_send.at[side * 2 + part], side_recv.at[side * 2 + part],
                device_id=device(peer), device_id_type=MESH,
            )
            copy.start()
            copies.append((copy, side, at))

    weights = jnp.broadcast_to(filled, (8, SLOTS)).astype(BF16)
    sums = jnp.dot(weights, table, preferred_element_type=F32)[:1]
    direction = sums * lax.rsqrt(jnp.sum(sums * sums, axis=1, keepdims=True) + EPS)
    high = direction.astype(BF16)
    rest = direction - high.astype(F32)
    middle = rest.astype(BF16)
    low = (rest - middle.astype(F32)).astype(BF16)
    row = iota((8, width), 0)
    parts = jnp.where(row == 2, low.astype(F32), 0.0)
    parts = jnp.where(row == 1, middle.astype(F32), parts)
    parts = jnp.where(row == 0, high.astype(F32), parts)
    central = jnp.sum(rows_dot(parts.astype(BF16), table), axis=0, keepdims=True)
    cent_ref[...] = jnp.where(filled > 0.5, central, 0.0)

    chunk = 256
    best = jnp.full((8, SLOTS), -1.0, F32)
    for first in range(0, SLOTS, chunk):
        scores = rows_dot(members[first : first + chunk], table)
        empty = members[first : first + chunk, :LANES][:, :1].astype(F32) > 1.5
        barred = empty | (iota((chunk, SLOTS), 0) + first == iota((chunk, SLOTS), 1))
        scores = jnp.where(barred, -1.0, scores)
        best = jnp.maximum(best, jnp.max(scores.reshape(chunk // 8, 8, SLOTS), axis=0))
    for copy, side, at in copies:
        copy.wait()
        scores = rows_dot(beside[at], table)
        top = jnp.max(scores.reshape(half // 8, 8, SLOTS), axis=0)
        there = me > 0 if side == 1 else me < DEVICES - 1
        best = jnp.maximum(best, jnp.where(there, top, -1.0))
    nearest = jnp.max(best, axis=0, keepdims=True)
    best_ref[...] = jnp.where(filled > 0.5, nearest, 0.0)
    return heads


def ranked(lab_ref):
    labels = lab_ref[...]
    rows = labels.shape[1]
    return labels, earlier_equal(labels.astype(F32), rows)


def four_slot_kernel(
    emb_hbm, lab_hbm, bnd_hbm, best_ref, cent_ref,
    emb_ref, lab_ref, bnd_ref, unit, out_buf, in_buf, members, picks, outward, beside,
    in_sem, stage_sem, send_sem, recv_sem, own_sem, side_send, side_recv,
):
    width = emb_ref.shape[1]
    here = place()
    me, _, my_z, _, _ = here
    got = fetch((emb_hbm, lab_hbm, bnd_hbm), (emb_ref, lab_ref, bnd_ref), in_sem)
    greet(me)
    for copy in got:
        copy.wait()
    labels, rank = ranked(lab_ref)
    normalise(emb_ref, unit)
    pass_on(me, stage_sem)
    build(labels.astype(F32) * CAP + rank, unit, out_buf, SLOTS, CAP)
    pl.semaphore_wait(stage_sem, SIDE - 1)
    own = pltpu.make_async_copy(out_buf.at[me], in_buf.at[me], own_sem)
    own.start()
    for dz in ORDER:
        send_group(here, dz, out_buf, in_buf, send_sem, recv_sem)
    turn_picks(bnd_ref, picks)
    own.wait()
    for dz in ORDER:
        awaited(me, in_buf, PLANE - 1 if dz == 0 else PLANE, send_sem, recv_sem.at[dz]).wait_recv()
        z = lax.rem(my_z + Z - dz, Z)
        for y in range(Y):
            first = (y * Z + z) * XC
            members[pl.ds(pl.multiple_of(first * CAP, XC * CAP), XC * CAP)] = in_buf[pl.ds(first, XC)].reshape(
                XC * CAP, width
            )
    finish(me, members, picks, outward, beside, side_send, side_recv, best_ref, cent_ref)
    awaited(me, out_buf, DEVICES - 1, send_sem, recv_sem.at[0]).wait_send()


def two_hop_kernel(
    emb_hbm, lab_hbm, bnd_hbm, best_ref, cent_ref, full_ref,
    emb_ref, lab_ref, bnd_ref, unit, out_buf, in_buf, members, picks, outward, beside,
    out_spill, in_spill, out_code, in_code, out_hop, in_hop,
    in_sem, stage_sem, send_sem, recv_sem, own_sem, side_send, side_recv,
    spill_send, spill_recv, code_send, code_recv, hop_send, hop_recv,
):
    rows, width = emb_ref.shape
    here = place()
    me, my_y, my_z, my_x, core = here
    mine = (my_y * X + my_x) * C + core
    got = fetch((emb_hbm, lab_hbm, bnd_hbm), (emb_ref, lab_ref, bnd_ref), in_sem)
    greet(me)
    got[1].wait()
    labels, rank = ranked(lab_ref)
    spilled = rank > DIRECT - 0.5
    plane = (labels >> 3) & (Z - 1)
    within = ((labels >> 6) << 3) | (labels & (XC - 1))
    key = jnp.where(spilled, plane, Z).astype(F32)
    spot = earlier_equal(key, rows)
    fits = spilled & (spot < SPILL - 0.5)
    full = jnp.max(jnp.where(spilled & (spot > SPILL - 0.5), 1.0, 0.0), axis=1, keepdims=True)
    direct_at = jnp.where(spilled, -1.0, labels.astype(F32) * DIRECT + rank)
    spill_at = jnp.where(fits, plane.astype(F32) * SPILL + spot, -1.0)
    code = within.astype(F32) * HOPPED + rank + (1 - DIRECT)
    got[0].wait()
    normalise(emb_ref, unit)
    pass_on(me, stage_sem)

    lines = Z * SPILL
    chosen = jnp.where(iota((lines, rows), 0).astype(F32) == spill_at, 1.0, 0.0)
    out_spill[...] = (
        jnp.dot(chosen.astype(BF16), unit[...], preferred_element_type=F32).astype(BF16).reshape(Z, SPILL, width)
    )
    codes = jnp.sum(chosen * code, axis=1, keepdims=True)
    out_code[...] = jnp.broadcast_to(codes, (lines, LANES)).astype(BF16).reshape(Z, SPILL, LANES)
    build(direct_at, unit, out_buf, DEVICES * DIRECT, DIRECT, full)
    pl.semaphore_wait(stage_sem, SIDE - 1)

    def over(i, _):
        z = lax.rem(my_z + i, Z)
        to = ((my_y * Z + z) * X + my_x, core)
        pltpu.make_async_remote_copy(
            out_code.at[z], in_code.at[my_z], code_send, code_recv, device_id=to, device_id_type=MESH
        ).start()
        pltpu.make_async_remote_copy(
            out_spill.at[z], in_spill.at[my_z], spill_send, spill_recv, device_id=to, device_id_type=MESH
        ).start()
        return 0

    lax.fori_loop(1, Z, over, 0)
    own = fetch(
        (out_buf.at[me], out_spill.at[my_z], out_code.at[my_z]),
        (in_buf.at[me], in_spill.at[my_z], in_code.at[my_z]),
        own_sem,
    )
    early = 3
    for dz in ORDER[:early]:
        send_group(here, dz, out_buf, in_buf, send_sem, recv_sem)
    got[2].wait()
    turn_picks(bnd_ref, picks)
    for copy in own:
        copy.wait()

    awaited(me, in_code, Z - 1, code_send, code_recv).wait_recv()
    awaited(me, in_spill, Z - 1, spill_send, spill_recv).wait_recv()
    told = in_code[...].reshape(lines, LANES).astype(F32).T
    told = told[:1]
    owner = jnp.floor((told - 0.5) * (1.0 / HOPPED))
    line = owner * (Z * HOPPED) + (iota((1, lines), 1) >> 4).astype(F32) * HOPPED + (told - 1.0 - owner * HOPPED)
    line = jnp.where(told > 0.5, line, -1.0)
    came = in_spill[...].reshape(lines, width)
    step = 128
    for i in range(PLANE * Z * HOPPED // step):
        chosen = jnp.where((iota((step, lines), 0) + i * step).astype(F32) == line, 1.0, 0.0)
        some = jnp.sum(chosen, axis=1, keepdims=True)
        block = jnp.dot(chosen.astype(BF16), came, preferred_element_type=F32)
        block = jnp.where((some < 0.5) & (iota((step, width), 1) == 0), EMPTY, block)
        each = Z * HOPPED
        out_hop[pl.ds(i * (step // each), step // each)] = block.astype(BF16).reshape(step // each, Z, HOPPED, width)

    def around(i, _):
        y, x, c = lax.rem(my_y + i // XC, Y), lax.rem(my_x + i // C, X), lax.rem(core + i, C)
        pltpu.make_async_remote_copy(
            out_hop.at[(y * X + x) * C + c], in_hop.at[mine], hop_send, hop_recv,
            device_id=((y * Z + my_z) * X + x, c), device_id_type=MESH,
        ).start()
        return 0

    lax.fori_loop(1, PLANE, around, 0)
    kept = pltpu.make_async_copy(out_hop.at[mine], in_hop.at[mine], own_sem.at[0])
    kept.start()
    for dz in ORDER[early:]:
        send_group(here, dz, out_buf, in_buf, send_sem, recv_sem)
    kept.wait()
    awaited(me, in_hop, PLANE - 1, hop_send, hop_recv).wait_recv()

    lines = PLANE * CAP
    a, b = iota((lines, lines), 0), iota((lines, lines), 1)
    k = a & (CAP - 1)
    source = (a >> 2) * DIRECT + (k & (DIRECT - 1)) + jnp.where(k >= DIRECT, PLANE * DIRECT, 0)
    mixing = jnp.where(source == b, 1.0, 0.0).astype(BF16)
    for dz in ORDER:
        awaited(me, in_buf, PLANE - 1 if dz == 0 else PLANE, send_sem, recv_sem.at[dz]).wait_recv()
        z = lax.rem(my_z + Z - dz, Z)
        blocks = [in_buf[pl.ds((y * Z + z) * XC, XC)].reshape(XC * DIRECT, width) for y in range(Y)]
        blocks.append(in_hop[:, z].reshape(PLANE * HOPPED, width))
        mixed = jnp.dot(mixing, jnp.concatenate(blocks, axis=0), preferred_element_type=F32).astype(BF16)
        for y in range(Y):
            first = (y * Z + z) * XC * CAP
            members[pl.ds(pl.multiple_of(first, XC * CAP), XC * CAP)] = mixed[y * XC * CAP : (y + 1) * XC * CAP]
    heads = finish(me, members, picks, outward, beside, side_send, side_recv, best_ref, cent_ref)
    full_ref[...] = jnp.broadcast_to(jnp.max(heads, axis=1, keepdims=True), full_ref.shape)

    awaited(me, out_buf, DEVICES - 1, send_sem, recv_sem.at[0]).wait_send()
    awaited(me, out_spill, Z - 1, spill_send, spill_recv).wait_send()
    awaited(me, out_code, Z - 1, code_send, code_recv).wait_send()
    awaited(me, out_hop, PLANE - 1, hop_send, hop_recv).wait_send()


def per_device(embeddings, cluster_ids, boundary_slots):
    rows, width = embeddings.shape
    bound = boundary_slots.shape[2]
    labels, ranks = cluster_ids.reshape(1, rows), boundary_slots[0]
    line = jax.ShapeDtypeStruct((1, SLOTS), F32)
    vmem, anywhere = pl.BlockSpec(memory_space=pltpu.VMEM), pl.BlockSpec(memory_space=pl.ANY)
    dma = pltpu.SemaphoreType.DMA

    def buffers(per):
        return [
            pltpu.VMEM((rows, width), F32),
            pltpu.VMEM((1, rows), jnp.int32),
            pltpu.VMEM((2, bound), jnp.int32),
            pltpu.VMEM((rows, width), BF16),
            pltpu.VMEM((DEVICES, per, width), BF16),
            pltpu.VMEM((DEVICES, per, width), BF16),
            pltpu.VMEM((SLOTS, width), BF16),
            pltpu.VMEM((2 * bound, LANES), F32),
            pltpu.VMEM((2 * bound, width), BF16),
            pltpu.VMEM((2 * bound, width), BF16),
        ]

    sems = [dma((3,)), pltpu.SemaphoreType.REGULAR, dma, dma((Z,))]

    def call(body, outs, scratch, number):
        return pl.pallas_call(
            body,
            out_shape=outs,
            in_specs=[anywhere] * 3,
            out_specs=(vmem,) * len(outs),
            scratch_shapes=scratch,
            compiler_params=pltpu.CompilerParams(
                collective_id=number, has_side_effects=True, vmem_limit_bytes=48 << 20
            ),
        )(embeddings, labels, ranks)

    best, central, full = call(
        two_hop_kernel,
        (line, line, jax.ShapeDtypeStruct((1, LANES), F32)),
        buffers(DIRECT)
        + [
            pltpu.VMEM((Z, SPILL, width), BF16),
            pltpu.VMEM((Z, SPILL, width), BF16),
            pltpu.VMEM((Z, SPILL, LANES), BF16),
            pltpu.VMEM((Z, SPILL, LANES), BF16),
            pltpu.VMEM((PLANE, Z, HOPPED, width), BF16),
            pltpu.VMEM((PLANE, Z, HOPPED, width), BF16),
        ]
        + sems
        + [dma((3,)), dma((4,)), dma((4,))]
        + [dma] * 6,
        0,
    )

    def again():
        return tuple(call(four_slot_kernel, (line, line), buffers(CAP) + sems + [dma, dma((4,)), dma((4,))], 1))

    return lax.cond(full[0, 0] > 4.0, again, lambda: (best, central))


def solution(mesh):
    placed = (P(("dp", "rep"), None), P(("dp", "rep"), None), P(("dp", "rep"), None, None))
    return jax.shard_map(
        per_device,
        mesh=mesh,
        in_specs=placed,
        out_specs=(P(("dp", "rep"), None), P(("dp", "rep"), None)),
        check_vma=False,
    )
```

time: 138 us -> 65.2 us (0.47)
  blocking collectives: 72.6 us -> 0 us
  Pallas kernels: 0 us -> 62.8 us
  other arithmetic: 15.4 us -> 0 us
  local copies, waits for them, and re-layouts: 16.3 us -> 1.2 us
  matrix products: 10.1 us -> 0 us
  starting transfers between devices: 9.77 us -> 0 us
  waiting for transfers between devices: 6.91 us -> 0 us
  loops' own time: 3.3 us -> 0.19 us
  between operations: 2.89 us -> 0.73 us
    all_to_all x2 -> x0, blocking collectives: 72.6 us -> none  [the longest x1 67.1 us: per_device(): lax.all_to_all(shaped, 'dp', split_axis=0, concat_axis=0, tiled=True)]
    pallas_call x0 -> x1, Pallas kernels: none -> 62.8 us  [call(): pl.pallas_call(body, out_shape=outs, in_specs=[anywhere] * 3, out_specs=(...]
    dot_general x4 -> x0, matrix products: 10.1 us -> none  [the longest x2 8.01 us: one_block(): lax.dot_general(block_rows, candidates, (((1,), (1,)), ((), ())), preferr...]
    ppermute x2 -> x0, starting transfers between devices: 9.77 us -> none  [from_behind(): return lax.ppermute(array, axis, pairs)]
    ppermute x2 -> x0, waiting for transfers between devices: 6.91 us -> none  [from_behind(): return lax.ppermute(array, axis, pairs)]
    reshape x2 -> x0, local copies, waits for them, and re-layouts: 5.27 us -> none  [the longest x1 2.73 us: per_device(): shaped = outgoing.reshape(n_chips, n_cores, capacity, width)]
    sort x1 -> x0, other arithmetic: 4.37 us -> none  [per_device(): order = jnp.argsort(1 - filled_int, stable=True)]
    gather x2 -> x0, local copies, waits for them, and re-layouts: 4.34 us -> none  [the longest x1 2.28 us: per_device(): positions = order[picks.reshape(-1)]]
  transfers between devices with their start and end apart: 2 -> 0, of which waited for: 2 -> 0; matrix products, arithmetic and copies ran while one was open for 0% -> 0% of each run, Pallas kernels for 0% -> 0%
where the time goes in v3:
time: 65.2 us; the launch traced here: 64.9 us
  Pallas kernels  62.8 us (96%)
  local copies, waits for them, and re-layouts  1.2 us (2%)
  between operations  0.73 us (1%)
    pallas_call x1, Pallas kernels, call(): pl.pallas_call(body, out_shape=outs, in_specs=[anywhere] * 3, out_specs=(...  62.8 us

profile of v3, /device:TPU:8, one launch (start us, length us, event | category | flops | bytes accessed | tf_op | source)
XLA Modules:
  0.0 64.9 jit_solution(17285008633605943568)
XLA Ops:
  0.6 0.0 copy-start
  0.6 0.0 copy-start.2
  0.6 0.0 copy-start.1
  0.7 62.8 %shard_map.54 = (f32[1,1024]{1,0:T(1,128)S(1)}, f32[1,1024]{1,0:T(1,128)S(1)}, f32[1,128]{1,0:T(1,128)S(1)}) custom-call(f32[512,1024]{1,0:T(8,128)} %emb_hbm.1, s32[1,512]{1,0:T(1,128)} %bitcast.5, s32[2,256]{1,0:T(2,128)} %bitcast.7), custom_call_target="tpu_custom_call" | custom-call | tf_op jit(solution)/shard_map/pallas_call | solution.py:410
  63.5 0.0 copy-done
  63.5 0.0 copy-done.2
  63.5 0.0 copy-done.1
  63.5 0.2 conditional.1
  63.7 0.6 copy.15
  64.3 0.6 copy.16
Async XLA Ops:
  0.6 62.9 %copy-start = (f32[512,1024]{1,0:T(8,128)S(1)}, f32[512,1024]{1,0:T(8,128)}, u32[]{:S(2)}) copy-start(f32[512,1024]{1,0:T(8,128)} %emb_hbm.1) | copy-start | bytes 6291460
  0.6 62.9 %copy-start.2 = (s32[1,2,256]{2,1,0:T(2,128)S(1)}, s32[1,2,256]{2,1,0:T(2,128)}, u32[]{:S(2)}) copy-start(s32[1,2,256]{2,1,0:T(2,128)} %param.7) | copy-start | bytes 6148
  0.6 62.9 %copy-start.1 = (s32[512,1]{0,1:T(1,128)S(1)}, s32[512,1]{0,1:T(1,128)}, u32[]{:S(2)}) copy-start(s32[512,1]{0,1:T(1,128)} %param.6) | copy-start | bytes 6148

commit v4 on v3

--- a/solution.py
+++ b/solution.py
@@ -22,7 +22,7 @@
 EPS = 1e-06
 EMPTY = 2.0
 FULL = 8.0
-ORDER = (4, 3, 5, 2, 6, 1, 7, 0)
+ORDER = (0, 1, 7, 2, 6, 4, 3, 5)
 F32 = jnp.float32
 BF16 = jnp.bfloat16
 
@@ -55,11 +55,13 @@
 
 
 def row_mate(me, i):
-    return me // SIDE * SIDE + lax.rem(me + i, SIDE)
+    y, z, x, c = me // (Z * XC), lax.rem(me // XC, Z), lax.rem(me // C, X), lax.rem(me, C)
+    return ((y * Z + lax.rem(z + i // C, Z)) * X + x) * C + lax.rem(c + i, C)
 
 
 def column_mate(me, i):
-    return lax.rem(me // SIDE + i, SIDE) * SIDE + lax.rem(me, SIDE)
+    y, z, x, c = me // (Z * XC), lax.rem(me // XC, Z), lax.rem(me // C, X), lax.rem(me, C)
+    return ((lax.rem(y + i // X, Y) * Z + z) * X + lax.rem(x + i, X)) * C + c
 
 
 def greet(me):
@@ -129,19 +131,32 @@
         picks[pl.ds(side * bound, bound)] = jnp.broadcast_to(raw[side : side + 1], (LANES, bound)).T
 
 
-def send_group(place_of_me, dz, source, target, send_sem, recv_sem):
-    me, my_y, my_z, my_x, core = place_of_me
-
+def in_plane(place_of_me, i):
+    _, my_y, _, my_x, core = place_of_me
+    return lax.rem(my_y + i // XC, Y), lax.rem(my_x + i // C, X), lax.rem(core + i, C)
+
+
+def send_one(place_of_me, dz, i, source, target, send_sem, recv_sem):
+    y, x, c = in_plane(place_of_me, i)
+    t = (y * Z + lax.rem(place_of_me[2] + dz, Z)) * X + x
+    pltpu.make_async_remote_copy(
+        source.at[t * C + c], target.at[place_of_me[0]], send_sem, recv_sem.at[dz],
+        device_id=(t, c), device_id_type=MESH,
+    ).start()
+
+
+def send_group(place_of_me, dzs, source, target, send_sem, recv_sem, beside=None):
     def one(i, _):
-        t = (lax.rem(my_y + i // XC, Y) * Z + lax.rem(my_z + dz, Z)) * X + lax.rem(my_x + i // C, X)
-        c = lax.rem(core + i, C)
-        pltpu.make_async_remote_copy(
-            source.at[t * C + c], target.at[me], send_sem, recv_sem.at[dz],
-            device_id=(t, c), device_id_type=MESH,
-        ).start()
-        return 0
-
-    lax.fori_loop(1 if dz == 0 else 0, PLANE, one, 0)
+        if beside is not None:
+            beside(i)
+        for dz in dzs:
+            send_one(place_of_me, dz, i, source, target, send_sem, recv_sem)
+        return 0
+
+    for dz in dzs:
+        if dz:
+            send_one(place_of_me, dz, 0, source, target, send_sem, recv_sem)
+    lax.fori_loop(1, PLANE, one, 0)
 
 
 def awaited(me, ref, n, send_sem, recv_sem):
@@ -247,7 +262,7 @@
     own = pltpu.make_async_copy(out_buf.at[me], in_buf.at[me], own_sem)
     own.start()
     for dz in ORDER:
-        send_group(here, dz, out_buf, in_buf, send_sem, recv_sem)
+        send_group(here, (dz,), out_buf, in_buf, send_sem, recv_sem)
     turn_picks(bnd_ref, picks)
     own.wait()
     for dz in ORDER:
@@ -287,9 +302,9 @@
     direct_at = jnp.where(spilled, -1.0, labels.astype(F32) * DIRECT + rank)
     spill_at = jnp.where(fits, plane.astype(F32) * SPILL + spot, -1.0)
     code = within.astype(F32) * HOPPED + rank + (1 - DIRECT)
+    pass_on(me, stage_sem)
     got[0].wait()
     normalise(emb_ref, unit)
-    pass_on(me, stage_sem)
 
     lines = Z * SPILL
     chosen = jnp.where(iota((lines, rows), 0).astype(F32) == spill_at, 1.0, 0.0)
@@ -298,8 +313,6 @@
     )
     codes = jnp.sum(chosen * code, axis=1, keepdims=True)
     out_code[...] = jnp.broadcast_to(codes, (lines, LANES)).astype(BF16).reshape(Z, SPILL, LANES)
-    build(direct_at, unit, out_buf, DEVICES * DIRECT, DIRECT, full)
-    pl.semaphore_wait(stage_sem, SIDE - 1)
 
     def over(i, _):
         z = lax.rem(my_z + i, Z)
@@ -313,14 +326,15 @@
         return 0
 
     lax.fori_loop(1, Z, over, 0)
+    build(direct_at, unit, out_buf, DEVICES * DIRECT, DIRECT, full)
+    pl.semaphore_wait(stage_sem, SIDE - 1)
     own = fetch(
         (out_buf.at[me], out_spill.at[my_z], out_code.at[my_z]),
         (in_buf.at[me], in_spill.at[my_z], in_code.at[my_z]),
         own_sem,
     )
-    early = 3
-    for dz in ORDER[:early]:
-        send_group(here, dz, out_buf, in_buf, send_sem, recv_sem)
+    early = 5
+    send_group(here, ORDER[:early], out_buf, in_buf, send_sem, recv_sem)
     got[2].wait()
     turn_picks(bnd_ref, picks)
     for copy in own:
@@ -343,19 +357,16 @@
         each = Z * HOPPED
         out_hop[pl.ds(i * (step // each), step // each)] = block.astype(BF16).reshape(step // each, Z, HOPPED, width)
 
-    def around(i, _):
-        y, x, c = lax.rem(my_y + i // XC, Y), lax.rem(my_x + i // C, X), lax.rem(core + i, C)
+    def around(i):
+        y, x, c = in_plane(here, i)
         pltpu.make_async_remote_copy(
             out_hop.at[(y * X + x) * C + c], in_hop.at[mine], hop_send, hop_recv,
             device_id=((y * Z + my_z) * X + x, c), device_id_type=MESH,
         ).start()
-        return 0
-
-    lax.fori_loop(1, PLANE, around, 0)
+
     kept = pltpu.make_async_copy(out_hop.at[mine], in_hop.at[mine], own_sem.at[0])
     kept.start()
-    for dz in ORDER[early:]:
-        send_group(here, dz, out_buf, in_buf, send_sem, recv_sem)
+    send_group(here, ORDER[early:], out_buf, in_buf, send_sem, recv_sem, around)
     kept.wait()
     awaited(me, in_hop, PLANE - 1, hop_send, hop_recv).wait_recv()
 

time: 65.2 us -> 61.2 us (0.939)
  Pallas kernels: 62.8 us -> 58.3 us
    pallas_call x1, Pallas kernels: 62.8 us -> 58.3 us  [call(): pl.pallas_call(body, out_shape=outs, in_specs=[anywhere] * 3, out_specs=(...]
where the time goes in v4:
time: 61.2 us; the launch traced here: 60.4 us
  Pallas kernels  58.3 us (95%)
  local copies, waits for them, and re-layouts  1.2 us (2%)
  between operations  0.73 us (1%)
    pallas_call x1, Pallas kernels, call(): pl.pallas_call(body, out_shape=outs, in_specs=[anywhere] * 3, out_specs=(...  58.3 us

profile of v4, /device:TPU:8, one launch (start us, length us, event | category | flops | bytes accessed | tf_op | source)
XLA Modules:
  0.0 60.4 jit_solution(8741039753970470418)
XLA Ops:
  0.6 0.0 copy-start
  0.6 0.0 copy-start.2
  0.6 0.0 copy-start.1
  0.7 58.3 %shard_map.54 = (f32[1,1024]{1,0:T(1,128)S(1)}, f32[1,1024]{1,0:T(1,128)S(1)}, f32[1,128]{1,0:T(1,128)S(1)}) custom-call(f32[512,1024]{1,0:T(8,128)} %emb_hbm.1, s32[1,512]{1,0:T(1,128)} %bitcast.5, s32[2,256]{1,0:T(2,128)} %bitcast.7), custom_call_target="tpu_custom_call" | custom-call | tf_op jit(solution)/shard_map/pallas_call | solution.py:421
  59.0 0.0 copy-done
  59.0 0.0 copy-done.2
  59.0 0.0 copy-done.1
  59.0 0.2 conditional.1
  59.2 0.6 copy.15
  59.8 0.6 copy.16
Async XLA Ops:
  0.6 58.4 %copy-start = (f32[512,1024]{1,0:T(8,128)S(1)}, f32[512,1024]{1,0:T(8,128)}, u32[]{:S(2)}) copy-start(f32[512,1024]{1,0:T(8,128)} %emb_hbm.1) | copy-start | bytes 6291460
  0.6 58.4 %copy-start.2 = (s32[1,2,256]{2,1,0:T(2,128)S(1)}, s32[1,2,256]{2,1,0:T(2,128)}, u32[]{:S(2)}) copy-start(s32[1,2,256]{2,1,0:T(2,128)} %param.7) | copy-start | bytes 6148
  0.6 58.4 %copy-start.1 = (s32[512,1]{0,1:T(1,128)S(1)}, s32[512,1]{0,1:T(1,128)}, u32[]{:S(2)}) copy-start(s32[512,1]{0,1:T(1,128)} %param.6) | copy-start | bytes 6148

commit v5 on v4

--- a/solution.py
+++ b/solution.py
@@ -23,6 +23,8 @@
 EMPTY = 2.0
 FULL = 8.0
 ORDER = (0, 1, 7, 2, 6, 4, 3, 5)
+EARLY = 5
+STRIDE = 13
 F32 = jnp.float32
 BF16 = jnp.bfloat16
 
@@ -133,6 +135,7 @@
 
 def in_plane(place_of_me, i):
     _, my_y, _, my_x, core = place_of_me
+    i = lax.rem(i * STRIDE, PLANE)
     return lax.rem(my_y + i // XC, Y), lax.rem(my_x + i // C, X), lax.rem(core + i, C)
 
 
@@ -166,45 +169,29 @@
     )
 
 
-def finish(me, members, picks, outward, beside, side_send, side_recv, best_ref, cent_ref):
-    width = members.shape[1]
-    bound = outward.shape[0] // 2
-    groups = SLOTS // LANES
-
+def exchange(me, part, rows, bound, outward, beside, side_send, side_recv):
+    half = bound // 2
+    side = 1 - part % 2
+    at = pl.ds(side * bound + part // 2 * half, half)
+    outward[at] = rows
+    peer = lax.rem(me + 1, DEVICES) if side == 1 else lax.rem(me + DEVICES - 1, DEVICES)
+    copy = pltpu.make_async_remote_copy(
+        outward.at[at], beside.at[at], side_send.at[part], side_recv.at[part],
+        device_id=device(peer), device_id_type=MESH,
+    )
+    copy.start()
+    return copy, side, at
+
+
+def filled_slots(members):
     corner = jnp.where(iota((8, LANES), 1) == 0, 1.0, 0.0).astype(BF16)
     heads = rows_dot(corner, members[:, :LANES])[:1]
-    filled = jnp.where(heads < 1.5, 1.0, 0.0)
-    stacked = jnp.concatenate([filled[:, k * LANES : (k + 1) * LANES] for k in range(groups)], axis=0)
-    upto = jnp.where(iota((LANES, LANES), 0) <= iota((LANES, LANES), 1), 1.0, 0.0).astype(BF16)
-    within = jnp.dot(stacked.astype(BF16), upto, preferred_element_type=F32)
-    totals = jnp.sum(stacked, axis=1, keepdims=True)
-    count = jnp.sum(totals, axis=0, keepdims=True)
-    order = []
-    before = jnp.zeros((1, 1), F32)
-    for k in range(groups):
-        order.append(jnp.where(stacked[k : k + 1] > 0.5, within[k : k + 1] + (before - 1.0), -1.0))
-        before = before + totals[k : k + 1]
-
-    half = bound // 2
-    above, below = lax.rem(me + 1, DEVICES), lax.rem(me + DEVICES - 1, DEVICES)
+    return heads, jnp.where(heads < 1.5, 1.0, 0.0)
+
+
+def close(me, members, filled, sums, copies, beside, best_ref, cent_ref):
+    width = members.shape[1]
     table = members[...]
-    copies = []
-    for part in range(2):
-        for side, peer in ((1, above), (0, below)):
-            at = pl.ds(side * bound + part * half, half)
-            want = picks[at]
-            want = want - jnp.floor((want + 0.5) / count) * count
-            chosen = [jnp.where(want == order[k], 1.0, 0.0).astype(BF16) for k in range(groups)]
-            outward[at] = jnp.dot(jnp.concatenate(chosen, axis=1), table, preferred_element_type=F32).astype(BF16)
-            copy = pltpu.make_async_remote_copy(
-                outward.at[at], beside.at[at], side_send.at[side * 2 + part], side_recv.at[side * 2 + part],
-                device_id=device(peer), device_id_type=MESH,
-            )
-            copy.start()
-            copies.append((copy, side, at))
-
-    weights = jnp.broadcast_to(filled, (8, SLOTS)).astype(BF16)
-    sums = jnp.dot(weights, table, preferred_element_type=F32)[:1]
     direction = sums * lax.rsqrt(jnp.sum(sums * sums, axis=1, keepdims=True) + EPS)
     high = direction.astype(BF16)
     rest = direction - high.astype(F32)
@@ -228,12 +215,42 @@
     for copy, side, at in copies:
         copy.wait()
         scores = rows_dot(beside[at], table)
-        top = jnp.max(scores.reshape(half // 8, 8, SLOTS), axis=0)
+        top = jnp.max(scores.reshape(at.size // 8, 8, SLOTS), axis=0)
         there = me > 0 if side == 1 else me < DEVICES - 1
         best = jnp.maximum(best, jnp.where(there, top, -1.0))
     nearest = jnp.max(best, axis=0, keepdims=True)
     best_ref[...] = jnp.where(filled > 0.5, nearest, 0.0)
-    return heads
+
+
+def wrapped(want, count):
+    return want - jnp.floor((want + 0.5) / count) * count
+
+
+def finish(me, members, picks, outward, beside, side_send, side_recv, best_ref, cent_ref):
+    bound = outward.shape[0] // 2
+    groups = SLOTS // LANES
+    _, filled = filled_slots(members)
+    stacked = jnp.concatenate([filled[:, k * LANES : (k + 1) * LANES] for k in range(groups)], axis=0)
+    upto = jnp.where(iota((LANES, LANES), 0) <= iota((LANES, LANES), 1), 1.0, 0.0).astype(BF16)
+    within = jnp.dot(stacked.astype(BF16), upto, preferred_element_type=F32)
+    totals = jnp.sum(stacked, axis=1, keepdims=True)
+    count = jnp.sum(totals, axis=0, keepdims=True)
+    order = []
+    before = jnp.zeros((1, 1), F32)
+    for k in range(groups):
+        order.append(jnp.where(stacked[k : k + 1] > 0.5, within[k : k + 1] + (before - 1.0), -1.0))
+        before = before + totals[k : k + 1]
+    table = members[...]
+    copies = []
+    half = bound // 2
+    for part in range(4):
+        want = wrapped(picks[pl.ds((1 - part % 2) * bound + part // 2 * half, half)], count)
+        chosen = [jnp.where(want == order[k], 1.0, 0.0).astype(BF16) for k in range(groups)]
+        rows = jnp.dot(jnp.concatenate(chosen, axis=1), table, preferred_element_type=F32).astype(BF16)
+        copies.append(exchange(me, part, rows, bound, outward, beside, side_send, side_recv))
+    weights = jnp.broadcast_to(filled, (8, SLOTS)).astype(BF16)
+    sums = jnp.dot(weights, table, preferred_element_type=F32)[:1]
+    close(me, members, filled, sums, copies, beside, best_ref, cent_ref)
 
 
 def ranked(lab_ref):
@@ -280,9 +297,9 @@
 def two_hop_kernel(
     emb_hbm, lab_hbm, bnd_hbm, best_ref, cent_ref, full_ref,
     emb_ref, lab_ref, bnd_ref, unit, out_buf, in_buf, members, picks, outward, beside,
-    out_spill, in_spill, out_code, in_code, out_hop, in_hop,
+    out_spill, in_spill, out_code, in_code, out_hop, in_hop, out_count, in_count, direct_pick, hop_pick, acc, direct,
     in_sem, stage_sem, send_sem, recv_sem, own_sem, side_send, side_recv,
-    spill_send, spill_recv, code_send, code_recv, hop_send, hop_recv,
+    spill_send, spill_recv, code_send, code_recv, hop_send, hop_recv, count_send, count_recv,
 ):
     rows, width = emb_ref.shape
     here = place()
@@ -311,8 +328,15 @@
     out_spill[...] = (
         jnp.dot(chosen.astype(BF16), unit[...], preferred_element_type=F32).astype(BF16).reshape(Z, SPILL, width)
     )
-    codes = jnp.sum(chosen * code, axis=1, keepdims=True)
-    out_code[...] = jnp.broadcast_to(codes, (lines, LANES)).astype(BF16).reshape(Z, SPILL, LANES)
+    lane = iota((rows, LANES), 1).astype(F32)
+    by_spot = jnp.where(along_sublanes(spot, LANES) == lane, 1.0, 0.0).astype(BF16)
+    by_owner = jnp.where(along_sublanes(within.astype(F32), LANES) + PLANE == lane, 1.0, 0.0).astype(BF16)
+    here_z = iota((Z, rows), 0) == plane
+    coded = jnp.where(here_z & fits, code, 0.0).astype(BF16)
+    counted = jnp.where(here_z, 1.0, 0.0).astype(BF16)
+    info = jnp.dot(coded, by_spot, preferred_element_type=F32)
+    info = info + jnp.dot(counted, by_owner, preferred_element_type=F32)
+    out_code[...] = jnp.broadcast_to(info[:, None, :], (Z, 8, LANES)).astype(BF16)
 
     def over(i, _):
         z = lax.rem(my_z + i, Z)
@@ -333,8 +357,7 @@
         (in_buf.at[me], in_spill.at[my_z], in_code.at[my_z]),
         own_sem,
     )
-    early = 5
-    send_group(here, ORDER[:early], out_buf, in_buf, send_sem, recv_sem)
+    send_group(here, ORDER[:EARLY], out_buf, in_buf, send_sem, recv_sem)
     got[2].wait()
     turn_picks(bnd_ref, picks)
     for copy in own:
@@ -342,8 +365,24 @@
 
     awaited(me, in_code, Z - 1, code_send, code_recv).wait_recv()
     awaited(me, in_spill, Z - 1, spill_send, spill_recv).wait_recv()
-    told = in_code[...].reshape(lines, LANES).astype(F32).T
-    told = told[:1]
+    info = jnp.max(in_code[...].astype(F32), axis=1)
+    turned = jnp.concatenate([info] * (LANES // Z), axis=0).T[PLANE : 2 * PLANE]
+    out_count[...] = jnp.broadcast_to(turned[:, None, :], (PLANE, 8, LANES)).astype(BF16)
+
+    def tell(i, _):
+        y, x, c = in_plane(here, i)
+        pltpu.make_async_remote_copy(
+            out_count.at[(y * X + x) * C + c], in_count.at[mine], count_send, count_recv,
+            device_id=((y * Z + my_z) * X + x, c), device_id_type=MESH,
+        ).start()
+        return 0
+
+    lax.fori_loop(1, PLANE, tell, 0)
+    noted = pltpu.make_async_copy(out_count.at[mine], in_count.at[mine], own_sem.at[1])
+    noted.start()
+    spread = jnp.where(iota((LANES, LANES), 0) == (iota((LANES, LANES), 1) & (SPILL - 1)), 1.0, 0.0).astype(BF16)
+    told = jnp.dot(info.astype(BF16), spread, preferred_element_type=F32)
+    told = jnp.sum(jnp.where(iota((Z, LANES), 0) == (iota((Z, LANES), 1) >> 4), told, 0.0), axis=0, keepdims=True)
     owner = jnp.floor((told - 0.5) * (1.0 / HOPPED))
     line = owner * (Z * HOPPED) + (iota((1, lines), 1) >> 4).astype(F32) * HOPPED + (told - 1.0 - owner * HOPPED)
     line = jnp.where(told > 0.5, line, -1.0)
@@ -355,7 +394,7 @@
         block = jnp.dot(chosen.astype(BF16), came, preferred_element_type=F32)
         block = jnp.where((some < 0.5) & (iota((step, width), 1) == 0), EMPTY, block)
         each = Z * HOPPED
-        out_hop[pl.ds(i * (step // each), step // each)] = block.astype(BF16).reshape(step // each, Z, HOPPED, width)
+        out_hop[pl.ds(i * (step // each), step // each)] = block.astype(BF16).reshape(step // each, each, width)
 
     def around(i):
         y, x, c = in_plane(here, i)
@@ -366,31 +405,114 @@
 
     kept = pltpu.make_async_copy(out_hop.at[mine], in_hop.at[mine], own_sem.at[0])
     kept.start()
-    send_group(here, ORDER[early:], out_buf, in_buf, send_sem, recv_sem, around)
+    send_group(here, ORDER[EARLY:], out_buf, in_buf, send_sem, recv_sem, around)
     kept.wait()
-    awaited(me, in_hop, PLANE - 1, hop_send, hop_recv).wait_recv()
-
-    lines = PLANE * CAP
-    a, b = iota((lines, lines), 0), iota((lines, lines), 1)
-    k = a & (CAP - 1)
-    source = (a >> 2) * DIRECT + (k & (DIRECT - 1)) + jnp.where(k >= DIRECT, PLANE * DIRECT, 0)
-    mixing = jnp.where(source == b, 1.0, 0.0).astype(BF16)
-    for dz in ORDER:
+    noted.wait()
+
+    awaited(me, in_count, PLANE - 1, count_send, count_recv).wait_recv()
+    bound = outward.shape[0] // 2
+    counts = jnp.max(in_count[...].astype(F32), axis=1)
+    a, b = iota((PLANE, PLANE), 0), iota((PLANE, PLANE), 1)
+    j, m = iota((LANES, LANES), 0), iota((LANES, LANES), 1)
+
+    def ones(mask):
+        return jnp.where(mask, 1.0, 0.0)
+
+    def small(left, right):
+        return jnp.dot(left.astype(BF16), right.astype(BF16), preferred_element_type=F32)
+
+    def exact(left, right):
+        return jnp.dot(left, right, precision=lax.Precision.HIGHEST, preferred_element_type=F32)
+
+    same_y = (a >> 3) == (b >> 3)
+    base = small(ones(same_y & (b < a)), counts)
+    base = base + small(small(ones(same_y), counts), ones((j < Z) & (j < (m & (Z - 1)))))
+    base = base + small(small(ones((b >> 3) < (a >> 3)), counts), ones(j < Z))
+    count = jnp.sum(jnp.where(iota((PLANE, LANES), 1) < Z, counts, 0.0), axis=1, keepdims=True)
+    count = jnp.sum(count, axis=0, keepdims=True)
+    want = wrapped(picks[...], count)
+
+    def standing(array):
+        return jnp.concatenate([array, jnp.zeros((LANES - PLANE, LANES), F32)], axis=0).T[:Z]
+
+    widen = ones((j == (m >> 1)) & (m < PLANE * DIRECT))
+    rank = (iota((Z, LANES), 1) & (DIRECT - 1)).astype(F32)
+    taken = rank < small(standing(counts), widen) - 0.5
+    order = jnp.where(taken, exact(standing(base), widen) + rank, -1.0)
+    taken = ones(taken)
+    for z in range(Z):
+        direct_pick[z, pl.ds(0, 2 * bound)] = ones(want == order[z : z + 1]).astype(BF16)
+        direct_pick[z, pl.ds(2 * bound, 16)] = jnp.broadcast_to(taken[z : z + 1], (16, LANES)).astype(BF16)
+
+    from_z = ones(j == ((m >> 1) & (Z - 1)))
+    own_xc = (iota((PLANE, LANES), 0) & (XC - 1)) == (iota((PLANE, LANES), 1) >> 4)
+
+    def folded(array):
+        return jnp.sum(jnp.where(own_xc, array, 0.0).reshape(Y, XC, LANES), axis=1)
+
+    rank = (iota((Y, LANES), 1) & (HOPPED - 1)).astype(F32) + DIRECT
+    taken = rank < folded(small(counts, from_z)) - 0.5
+    order = jnp.where(taken, folded(exact(base, from_z)) + rank, -1.0)
+    taken = ones(taken)
+    for y in range(Y):
+        at = pl.ds(y * LANES, LANES)
+        hop_pick[pl.ds(0, 2 * bound), at] = ones(want == order[y : y + 1]).astype(BF16)
+        hop_pick[pl.ds(2 * bound, 16), at] = jnp.broadcast_to(taken[y : y + 1], (16, LANES)).astype(BF16)
+
+    each = PLANE * DIRECT
+
+    def settle(dz):
         awaited(me, in_buf, PLANE - 1 if dz == 0 else PLANE, send_sem, recv_sem.at[dz]).wait_recv()
         z = lax.rem(my_z + Z - dz, Z)
-        blocks = [in_buf[pl.ds((y * Z + z) * XC, XC)].reshape(XC * DIRECT, width) for y in range(Y)]
-        blocks.append(in_hop[:, z].reshape(PLANE * HOPPED, width))
-        mixed = jnp.dot(mixing, jnp.concatenate(blocks, axis=0), preferred_element_type=F32).astype(BF16)
         for y in range(Y):
-            first = (y * Z + z) * XC * CAP
-            members[pl.ds(pl.multiple_of(first, XC * CAP), XC * CAP)] = mixed[y * XC * CAP : (y + 1) * XC * CAP]
-    heads = finish(me, members, picks, outward, beside, side_send, side_recv, best_ref, cent_ref)
+            direct[z, pl.ds(y * XC * DIRECT, XC * DIRECT)] = in_buf[pl.ds((y * Z + z) * XC, XC)].reshape(
+                XC * DIRECT, width
+            )
+        return z
+
+    for n, dz in enumerate(ORDER[:EARLY]):
+        z = settle(dz)
+        given = jnp.dot(direct_pick[z][:, :each], direct[z], preferred_element_type=F32)
+        acc[...] = given if n == 0 else acc[...] + given
+    awaited(me, in_hop, PLANE - 1, hop_send, hop_recv).wait_recv()
+    hopped = in_hop[...].reshape(PLANE * Z * HOPPED, width)
+    acc[...] += jnp.dot(hop_pick[...], hopped, preferred_element_type=F32)
+    planes = [settle(dz) for dz in ORDER[EARLY:]]
+    latest = jnp.concatenate([direct[z] for z in planes], axis=0)
+
+    def gather(first, size):
+        at = pl.ds(first, size)
+        chosen = jnp.concatenate([direct_pick[z, at][:, :each] for z in planes], axis=1)
+        return acc[at] + jnp.dot(chosen, latest, preferred_element_type=F32)
+
+    half = bound // 2
+    copies = []
+    for part in range(4):
+        rows_out = gather((1 - part % 2) * bound + part // 2 * half, half).astype(BF16)
+        copies.append(exchange(me, part, rows_out, bound, outward, beside, side_send, side_recv))
+    sums = gather(2 * bound, 16)[:1]
+
+    lines = PLANE * CAP
+    a, b = iota((lines, each), 0), iota((lines, each), 1)
+    k = a & (CAP - 1)
+    from_direct = ones((k < DIRECT) & (b == (a >> 2) * DIRECT + k)).astype(BF16)
+    a, b = iota((lines, PLANE * Z * HOPPED), 0), iota((lines, PLANE * Z * HOPPED), 1)
+    k = a & (CAP - 1)
+    for z in range(Z):
+        from_hop = ones((k >= DIRECT) & (b == (a >> 2) * (Z * HOPPED) + z * HOPPED + k - DIRECT)).astype(BF16)
+        mixed = jnp.dot(from_direct, direct[z], preferred_element_type=F32)
+        mixed = (mixed + jnp.dot(from_hop, hopped, preferred_element_type=F32)).astype(BF16)
+        for y in range(Y):
+            members[pl.ds((y * Z + z) * XC * CAP, XC * CAP)] = mixed[y * XC * CAP : (y + 1) * XC * CAP]
+    heads, filled = filled_slots(members)
+    close(me, members, filled, sums, copies, beside, best_ref, cent_ref)
     full_ref[...] = jnp.broadcast_to(jnp.max(heads, axis=1, keepdims=True), full_ref.shape)
 
     awaited(me, out_buf, DEVICES - 1, send_sem, recv_sem.at[0]).wait_send()
     awaited(me, out_spill, Z - 1, spill_send, spill_recv).wait_send()
     awaited(me, out_code, Z - 1, code_send, code_recv).wait_send()
     awaited(me, out_hop, PLANE - 1, hop_send, hop_recv).wait_send()
+    awaited(me, out_count, PLANE - 1, count_send, count_recv).wait_send()
 
 
 def per_device(embeddings, cluster_ids, boundary_slots):
@@ -436,14 +558,20 @@
         + [
             pltpu.VMEM((Z, SPILL, width), BF16),
             pltpu.VMEM((Z, SPILL, width), BF16),
-            pltpu.VMEM((Z, SPILL, LANES), BF16),
-            pltpu.VMEM((Z, SPILL, LANES), BF16),
-            pltpu.VMEM((PLANE, Z, HOPPED, width), BF16),
-            pltpu.VMEM((PLANE, Z, HOPPED, width), BF16),
+            pltpu.VMEM((Z, 8, LANES), BF16),
+            pltpu.VMEM((Z, 8, LANES), BF16),
+            pltpu.VMEM((PLANE, Z * HOPPED, width), BF16),
+            pltpu.VMEM((PLANE, Z * HOPPED, width), BF16),
+            pltpu.VMEM((PLANE, 8, LANES), BF16),
+            pltpu.VMEM((PLANE, 8, LANES), BF16),
+            pltpu.VMEM((Z, 2 * bound + 16, LANES), BF16),
+            pltpu.VMEM((2 * bound + 16, PLANE * Z * HOPPED), BF16),
+            pltpu.VMEM((2 * bound + 16, width), F32),
+            pltpu.VMEM((Z, PLANE * DIRECT, width), BF16),
         ]
         + sems
         + [dma((3,)), dma((4,)), dma((4,))]
-        + [dma] * 6,
+        + [dma] * 8,
         0,
     )
 

time: 61.2 us -> 57.9 us (0.946); the launches traced: 60.4 us -> 57.8 us
  Pallas kernels: 58.3 us -> 55.7 us
    pallas_call x1, Pallas kernels: 58.3 us -> 55.7 us  [call(): pl.pallas_call(body, out_shape=outs, in_specs=[anywhere] * 3, out_specs=(...]
where the time goes in v5:
time: 57.9 us; the launch traced here: 57.8 us
  Pallas kernels  55.7 us (96%)
  local copies, waits for them, and re-layouts  1.2 us (2%)
  between operations  0.73 us (1%)
    pallas_call x1, Pallas kernels, call(): pl.pallas_call(body, out_shape=outs, in_specs=[anywhere] * 3, out_specs=(...  55.7 us
    unnamed x8, local copies, waits for them, and re-layouts  1.2 us

profile of v5, /device:TPU:8, one launch (start us, length us, event | category | flops | bytes accessed | tf_op | source)
XLA Modules:
  0.0 57.8 jit_solution(522161714303021348)
XLA Ops:
  0.6 0.0 copy-start
  0.6 0.0 copy-start.2
  0.6 0.0 copy-start.1
  0.7 55.7 %shard_map.54 = (f32[1,1024]{1,0:T(1,128)S(1)}, f32[1,1024]{1,0:T(1,128)S(1)}, f32[1,128]{1,0:T(1,128)S(1)}) custom-call(f32[512,1024]{1,0:T(8,128)} %emb_hbm.1, s32[1,512]{1,0:T(1,128)} %bitcast.5, s32[2,256]{1,0:T(2,128)} %bitcast.7), custom_call_target="tpu_custom_call" | custom-call | tf_op jit(solution)/shard_map/pallas_call | solution.py:543
  56.4 0.0 copy-done
  56.4 0.0 copy-done.2
  56.4 0.0 copy-done.1
  56.4 0.2 conditional.1
  56.6 0.6 %copy.15 = f32[1,1024]{1,0:T(1,128)} copy(f32[1,1024]{1,0:T(1,128)S(1)} %get-tuple-element.33) | data formatting | bytes 8192
  57.2 0.6 %copy.16 = f32[1,1024]{1,0:T(1,128)} copy(f32[1,1024]{1,0:T(1,128)S(1)} %get-tuple-element.34) | data formatting | bytes 8192
Async XLA Ops:
  0.6 55.8 %copy-start = (f32[512,1024]{1,0:T(8,128)S(1)}, f32[512,1024]{1,0:T(8,128)}, u32[]{:S(2)}) copy-start(f32[512,1024]{1,0:T(8,128)} %emb_hbm.1) | copy-start | bytes 6291460
  0.6 55.8 %copy-start.2 = (s32[1,2,256]{2,1,0:T(2,128)S(1)}, s32[1,2,256]{2,1,0:T(2,128)}, u32[]{:S(2)}) copy-start(s32[1,2,256]{2,1,0:T(2,128)} %param.7) | copy-start | bytes 6148
  0.6 55.8 %copy-start.1 = (s32[512,1]{0,1:T(1,128)S(1)}, s32[512,1]{0,1:T(1,128)}, u32[]{:S(2)}) copy-start(s32[512,1]{0,1:T(1,128)} %param.6) | copy-start | bytes 6148

commit v6 on v5

--- a/solution.py
+++ b/solution.py
@@ -319,7 +319,6 @@
     direct_at = jnp.where(spilled, -1.0, labels.astype(F32) * DIRECT + rank)
     spill_at = jnp.where(fits, plane.astype(F32) * SPILL + spot, -1.0)
     code = within.astype(F32) * HOPPED + rank + (1 - DIRECT)
-    pass_on(me, stage_sem)
     got[0].wait()
     normalise(emb_ref, unit)
 
@@ -337,9 +336,10 @@
     info = jnp.dot(coded, by_spot, preferred_element_type=F32)
     info = info + jnp.dot(counted, by_owner, preferred_element_type=F32)
     out_code[...] = jnp.broadcast_to(info[:, None, :], (Z, 8, LANES)).astype(BF16)
-
-    def over(i, _):
-        z = lax.rem(my_z + i, Z)
+    pass_on(me, stage_sem)
+
+    def over(dz):
+        z = lax.rem(my_z + dz, Z)
         to = ((my_y * Z + z) * X + my_x, core)
         pltpu.make_async_remote_copy(
             out_code.at[z], in_code.at[my_z], code_send, code_recv, device_id=to, device_id_type=MESH
@@ -347,9 +347,9 @@
         pltpu.make_async_remote_copy(
             out_spill.at[z], in_spill.at[my_z], spill_send, spill_recv, device_id=to, device_id_type=MESH
         ).start()
-        return 0
-
-    lax.fori_loop(1, Z, over, 0)
+
+    for dz in (4, 3, 5, 2, 6, 1, 7):
+        over(dz)
     build(direct_at, unit, out_buf, DEVICES * DIRECT, DIRECT, full)
     pl.semaphore_wait(stage_sem, SIDE - 1)
     own = fetch(

time: 57.9 us -> 57 us (0.984)
  Pallas kernels: 55.7 us -> 54.8 us
    pallas_call x1, Pallas kernels: 55.7 us -> 54.8 us  [call(): pl.pallas_call(body, out_shape=outs, in_specs=[anywhere] * 3, out_specs=(...]
where the time goes in v6:
time: 57 us; the launch traced here: 56.9 us
  Pallas kernels  54.8 us (96%)
  local copies, waits for them, and re-layouts  1.2 us (2%)
  between operations  0.73 us (1%)
    pallas_call x1, Pallas kernels, call(): pl.pallas_call(body, out_shape=outs, in_specs=[anywhere] * 3, out_specs=(...  54.8 us
    unnamed x8, local copies, waits for them, and re-layouts  1.2 us

profile of v6, /device:TPU:8, one launch (start us, length us, event | category | flops | bytes accessed | tf_op | source)
XLA Modules:
  0.0 56.9 jit_solution(14496554952294757539)
XLA Ops:
  0.6 0.0 copy-start
  0.6 0.0 copy-start.2
  0.6 0.0 copy-start.1
  0.7 54.8 %shard_map.54 = (f32[1,1024]{1,0:T(1,128)S(1)}, f32[1,1024]{1,0:T(1,128)S(1)}, f32[1,128]{1,0:T(1,128)S(1)}) custom-call(f32[512,1024]{1,0:T(8,128)} %emb_hbm.1, s32[1,512]{1,0:T(1,128)} %bitcast.5, s32[2,256]{1,0:T(2,128)} %bitcast.7), custom_call_target="tpu_custom_call" | custom-call | tf_op jit(solution)/shard_map/pallas_call | solution.py:543
  55.5 0.0 copy-done
  55.5 0.0 copy-done.2
  55.5 0.0 copy-done.1
  55.5 0.2 conditional.1
  55.7 0.6 %copy.15 = f32[1,1024]{1,0:T(1,128)} copy(f32[1,1024]{1,0:T(1,128)S(1)} %get-tuple-element.33) | data formatting | bytes 8192
  56.3 0.6 %copy.16 = f32[1,1024]{1,0:T(1,128)} copy(f32[1,1024]{1,0:T(1,128)S(1)} %get-tuple-element.34) | data formatting | bytes 8192
Async XLA Ops:
  0.6 54.9 %copy-start = (f32[512,1024]{1,0:T(8,128)S(1)}, f32[512,1024]{1,0:T(8,128)}, u32[]{:S(2)}) copy-start(f32[512,1024]{1,0:T(8,128)} %emb_hbm.1) | copy-start | bytes 6291460
  0.6 54.9 %copy-start.2 = (s32[1,2,256]{2,1,0:T(2,128)S(1)}, s32[1,2,256]{2,1,0:T(2,128)}, u32[]{:S(2)}) copy-start(s32[1,2,256]{2,1,0:T(2,128)} %param.7) | copy-start | bytes 6148
  0.6 54.9 %copy-start.1 = (s32[512,1]{0,1:T(1,128)S(1)}, s32[512,1]{0,1:T(1,128)}, u32[]{:S(2)}) copy-start(s32[512,1]{0,1:T(1,128)} %param.6) | copy-start | bytes 6148

commit v7 on v6

--- a/solution.py
+++ b/solution.py
@@ -189,19 +189,21 @@
     return heads, jnp.where(heads < 1.5, 1.0, 0.0)
 
 
-def close(me, members, filled, sums, copies, beside, best_ref, cent_ref):
-    width = members.shape[1]
-    table = members[...]
+def split_centre(sums, lines):
     direction = sums * lax.rsqrt(jnp.sum(sums * sums, axis=1, keepdims=True) + EPS)
     high = direction.astype(BF16)
     rest = direction - high.astype(F32)
     middle = rest.astype(BF16)
     low = (rest - middle.astype(F32)).astype(BF16)
-    row = iota((8, width), 0)
+    row = iota((lines, sums.shape[1]), 0)
     parts = jnp.where(row == 2, low.astype(F32), 0.0)
     parts = jnp.where(row == 1, middle.astype(F32), parts)
-    parts = jnp.where(row == 0, high.astype(F32), parts)
-    central = jnp.sum(rows_dot(parts.astype(BF16), table), axis=0, keepdims=True)
+    return jnp.where(row == 0, high.astype(F32), parts).astype(BF16)
+
+
+def close(me, members, filled, sums, copies, beside, best_ref, cent_ref):
+    table = members[...]
+    central = jnp.sum(rows_dot(split_centre(sums, 8), table), axis=0, keepdims=True)
     cent_ref[...] = jnp.where(filled > 0.5, central, 0.0)
 
     chunk = 256
@@ -296,7 +298,7 @@
 
 def two_hop_kernel(
     emb_hbm, lab_hbm, bnd_hbm, best_ref, cent_ref, full_ref,
-    emb_ref, lab_ref, bnd_ref, unit, out_buf, in_buf, members, picks, outward, beside,
+    emb_ref, lab_ref, bnd_ref, unit, out_buf, in_buf, turn, picks, outward, beside,
     out_spill, in_spill, out_code, in_code, out_hop, in_hop, out_count, in_count, direct_pick, hop_pick, acc, direct,
     in_sem, stage_sem, send_sem, recv_sem, own_sem, side_send, side_recv,
     spill_send, spill_recv, code_send, code_recv, hop_send, hop_recv, count_send, count_recv,
@@ -460,6 +462,15 @@
         hop_pick[pl.ds(2 * bound, 16), at] = jnp.broadcast_to(taken[y : y + 1], (16, LANES)).astype(BF16)
 
     each = PLANE * DIRECT
+    step = 128
+    for first in range(0, SLOTS, step):
+        i = iota((step, 1), 0) + first
+        if first < SLOTS // 2:
+            z, y, xc, k = i >> 6, (i >> 4) & (Y - 1), (i >> 1) & (XC - 1), i & (DIRECT - 1)
+        else:
+            y, xc, z, k = (i >> 7) & (Y - 1), (i >> 4) & (XC - 1), (i >> 1) & (Z - 1), (i & (HOPPED - 1)) + DIRECT
+        slot = ((y * Z + z) * XC + xc) * CAP + k
+        turn[pl.ds(first, step)] = ones(slot == iota((step, SLOTS), 1)).astype(BF16)
 
     def settle(dz):
         awaited(me, in_buf, PLANE - 1 if dz == 0 else PLANE, send_sem, recv_sem.at[dz]).wait_recv()
@@ -486,26 +497,76 @@
         return acc[at] + jnp.dot(chosen, latest, preferred_element_type=F32)
 
     half = bound // 2
+    above, below = lax.rem(me + 1, DEVICES), lax.rem(me + DEVICES - 1, DEVICES)
     copies = []
-    for part in range(4):
-        rows_out = gather((1 - part % 2) * bound + part // 2 * half, half).astype(BF16)
-        copies.append(exchange(me, part, rows_out, bound, outward, beside, side_send, side_recv))
+    for part, (side, peer, skip, size) in enumerate(
+        (
+            (core, jnp.where(core == 1, above, below), 0, half),
+            (core, jnp.where(core == 1, above, below), half, half),
+            (1 - core, jnp.where(core == 1, below, above), 0, bound),
+        )
+    ):
+        first = pl.multiple_of(side * bound + skip, half)
+        outward[pl.ds(first, size)] = gather(first, size).astype(BF16)
+        view = pl.ds(first, size)
+        copy = pltpu.make_async_remote_copy(
+            outward.at[view], beside.at[view], side_send.at[part], side_recv.at[part],
+            device_id=device(peer), device_id_type=MESH,
+        )
+        copy.start()
+        copies.append(copy)
     sums = gather(2 * bound, 16)[:1]
 
-    lines = PLANE * CAP
-    a, b = iota((lines, each), 0), iota((lines, each), 1)
-    k = a & (CAP - 1)
-    from_direct = ones((k < DIRECT) & (b == (a >> 2) * DIRECT + k)).astype(BF16)
-    a, b = iota((lines, PLANE * Z * HOPPED), 0), iota((lines, PLANE * Z * HOPPED), 1)
-    k = a & (CAP - 1)
-    for z in range(Z):
-        from_hop = ones((k >= DIRECT) & (b == (a >> 2) * (Z * HOPPED) + z * HOPPED + k - DIRECT)).astype(BF16)
-        mixed = jnp.dot(from_direct, direct[z], preferred_element_type=F32)
-        mixed = (mixed + jnp.dot(from_hop, hopped, preferred_element_type=F32)).astype(BF16)
-        for y in range(Y):
-            members[pl.ds((y * Z + z) * XC * CAP, XC * CAP)] = mixed[y * XC * CAP : (y + 1) * XC * CAP]
-    heads, filled = filled_slots(members)
-    close(me, members, filled, sums, copies, beside, best_ref, cent_ref)
+    part_size = SLOTS // 2
+    tables = (direct[...].reshape(part_size, width), hopped)
+    chunk = 512
+    halves = []
+    for own_table in tables:
+        most = jnp.full((8, part_size), -1.0, F32)
+        for table in tables:
+            for first in range(0, part_size, chunk):
+                cand = table[first : first + chunk]
+                scores = rows_dot(cand, own_table)
+                barred = cand[:, :LANES][:, :1].astype(F32) > 1.5
+                if table is own_table:
+                    barred = barred | (iota((chunk, part_size), 0) + first == iota((chunk, part_size), 1))
+                scores = jnp.where(barred, -1.0, scores)
+                most = jnp.maximum(most, jnp.max(scores.reshape(chunk // 8, 8, part_size), axis=0))
+        halves.append(most)
+    corner = jnp.where(iota((8, LANES), 1) == 0, 1.0, 0.0).astype(BF16)
+    heads = jnp.concatenate([rows_dot(corner, table[:, :LANES])[:1] for table in tables], axis=1)
+    centre = split_centre(sums, 16)
+    central = []
+    off_chip = (me > 0) & (me < DEVICES - 1)
+    inner = pl.multiple_of(core * bound, bound)
+    outer = pl.multiple_of((1 - core) * bound, bound)
+    copies[2].wait()
+    copies[0].wait()
+    rows_in = jnp.concatenate([beside[pl.ds(inner, bound)], beside[pl.ds(outer, half)], centre], axis=0)
+    for n, table in enumerate(tables):
+        scores = rows_dot(rows_in, table)
+        near = jnp.max(scores[:bound].reshape(bound // 8, 8, part_size), axis=0)
+        far = jnp.max(scores[bound : bound + half].reshape(half // 8, 8, part_size), axis=0)
+        halves[n] = jnp.maximum(halves[n], jnp.maximum(near, jnp.where(off_chip, far, -1.0)))
+        central.append(jnp.sum(scores[bound + half : bound + half + 8], axis=0, keepdims=True))
+    copies[1].wait()
+    rows_in = beside[pl.ds(pl.multiple_of(outer + half, half), half)]
+    for n, table in enumerate(tables):
+        far = jnp.max(rows_dot(rows_in, table).reshape(half // 8, 8, part_size), axis=0)
+        halves[n] = jnp.maximum(halves[n], jnp.where(off_chip, far, -1.0))
+    nearest = jnp.max(jnp.concatenate(halves, axis=1), axis=0, keepdims=True)
+    central = jnp.concatenate(central, axis=1)
+
+    row = iota((8, SLOTS), 0)
+    both = jnp.where(row < 4, nearest, central)
+    both = jnp.where(heads < 1.5, both, 0.0)
+    high = both.astype(BF16).astype(F32)
+    middle = (both - high).astype(BF16).astype(F32)
+    low = both - high - middle
+    both = jnp.where((row & 3) == 0, high, jnp.where((row & 3) == 1, middle, jnp.where((row & 3) == 2, low, 0.0)))
+    both = jnp.dot(both.astype(BF16), turn[...], preferred_element_type=F32)
+    best_ref[...] = jnp.sum(both[:4], axis=0, keepdims=True)
+    cent_ref[...] = jnp.sum(both[4:], axis=0, keepdims=True)
     full_ref[...] = jnp.broadcast_to(jnp.max(heads, axis=1, keepdims=True), full_ref.shape)
 
     awaited(me, out_buf, DEVICES - 1, send_sem, recv_sem.at[0]).wait_send()

time: 57 us -> 56.5 us (level)
  no operation moved by 1% of the time
where the time goes in v7:
time: 56.5 us; the launch traced here: 56.4 us
  Pallas kernels  54.3 us (96%)
  local copies, waits for them, and re-layouts  1.2 us (2%)
  between operations  0.73 us (1%)
    pallas_call x1, Pallas kernels, call(): pl.pallas_call(body, out_shape=outs, in_specs=[anywhere] * 3, out_specs=(...  54.3 us
    unnamed x8, local copies, waits for them, and re-layouts  1.2 us

profile of v7, /device:TPU:8, one launch (start us, length us, event | category | flops | bytes accessed | tf_op | source)
XLA Modules:
  0.0 56.4 jit_solution(18089877328277555514)
XLA Ops:
  0.6 0.0 copy-start
  0.6 0.0 copy-start.2
  0.6 0.0 copy-start.1
  0.7 54.3 %shard_map.54 = (f32[1,1024]{1,0:T(1,128)S(1)}, f32[1,1024]{1,0:T(1,128)S(1)}, f32[1,128]{1,0:T(1,128)S(1)}) custom-call(f32[512,1024]{1,0:T(8,128)} %emb_hbm.1, s32[1,512]{1,0:T(1,128)} %bitcast.5, s32[2,256]{1,0:T(2,128)} %bitcast.7), custom_call_target="tpu_custom_call" | custom-call | tf_op jit(solution)/shard_map/pallas_call | solution.py:604
  55.0 0.0 copy-done
  55.0 0.0 copy-done.2
  55.0 0.0 copy-done.1
  55.0 0.2 conditional.1
  55.2 0.6 %copy.15 = f32[1,1024]{1,0:T(1,128)} copy(f32[1,1024]{1,0:T(1,128)S(1)} %get-tuple-element.33) | data formatting | bytes 8192
  55.8 0.6 %copy.16 = f32[1,1024]{1,0:T(1,128)} copy(f32[1,1024]{1,0:T(1,128)S(1)} %get-tuple-element.34) | data formatting | bytes 8192
Async XLA Ops:
  0.6 54.4 %copy-start = (f32[512,1024]{1,0:T(8,128)S(1)}, f32[512,1024]{1,0:T(8,128)}, u32[]{:S(2)}) copy-start(f32[512,1024]{1,0:T(8,128)} %emb_hbm.1) | copy-start | bytes 6291460
  0.6 54.4 %copy-start.2 = (s32[1,2,256]{2,1,0:T(2,128)S(1)}, s32[1,2,256]{2,1,0:T(2,128)}, u32[]{:S(2)}) copy-start(s32[1,2,256]{2,1,0:T(2,128)} %param.7) | copy-start | bytes 6148
  0.6 54.4 %copy-start.1 = (s32[512,1]{0,1:T(1,128)S(1)}, s32[512,1]{0,1:T(1,128)}, u32[]{:S(2)}) copy-start(s32[512,1]{0,1:T(1,128)} %param.6) | copy-start | bytes 6148
